TPU v7x, 128 devices: a whole 4x4x4 slice. The times are simulated.
128 devices in a mesh: tok: 8 (over z, core), head: 16 (over y, x).
Axes of the slice: x: 4, y: 4, z: 4, core: 2. Of those that a mesh axis runs over, the one named last changes fastest.
Arguments:
- stream: bfloat16 [2048, 7168], P('tok'), may hold values from -400 to 400
- row_tree_nodes: int32 [2048], replicated, may hold values from 0 to 2047, as said below
- input_norm_gain: bfloat16 [7168], replicated, may hold values from 0.099609375 to 1.8984375
- query_key_value_weight: bfloat16 [7168, 3, 7168], P('head', None, 'tok'), may hold values from -0.141736677 to 0.141736677
- adapter_down_weight: bfloat16 [7168, 128], replicated, may hold values from -0.0625 to 0.0625
- adapter_up_weight: bfloat16 [128, 3, 7168], P('head', None, 'tok'), may hold values from -0.23925781 to 0.23925781
- key_value_cache: bfloat16 [2, 32, 2048, 7168], P(None, 'head', None, 'tok'), may hold values from -104 to 104
- cache_length: int32 [32], P('head'), may hold values from 256 to 2048, as said below
- parents: int32 [32, 64], P('head'), may hold values from 0 to 62, as said below
- accepted: int32 [32, 8], P('head'), may hold values from 0 to 63, as said below
- output_weight: bfloat16 [7168, 3584], P('tok', 'head'), may hold values from -0.375 to 0.375
Outputs:
- attended: bfloat16 [2048, 3584], P('tok', 'head')
- accepted_kv: bfloat16 [2, 32, 8, 7168], P(None, 'head', None, 'tok')
Inputs may be any that keep to these rules, and one draw needn't show every extreme that they name: row_tree_nodes is a permutation of the 2048 node numbers; every aligned block of 128 rows holds exactly 4 nodes of every request. `cache_length`: at least one request's cache holds exactly 2048 positions. parents[r, 0] = 0 marks the root; parents[r, n] < n for n > 0. `accepted`: each row lists 8 nodes of its request's tree, each the parent of the next.
All inputs are finite; a program needn't handle non-finite values.
Results may differ from a plain program's by a relative error of at most 0.014.
Values may be sent and summed in bfloat16 or wider, within the bound.
A program may use at most 192 MiB of HBM per device.

v0:
```python
import jax
import jax.numpy as jnp
from jax import lax
from jax.sharding import PartitionSpec as P

HEAD_SIZE = 224
NODES = 64


def ancestors_of(parents):
    parent_links = jax.nn.one_hot(parents, NODES, dtype=jnp.float32)
    identity_matrix = jnp.eye(NODES, dtype=jnp.float32)
    ancestry = jnp.minimum(identity_matrix[None] + parent_links, 1.0)
    for squaring in range(NODES.bit_length()):
        ancestry = jnp.minimum(
            jnp.einsum("rnm,rmk->rnk", ancestry, ancestry, precision=lax.Precision.HIGHEST), 1.0
        )
    return ancestry


def on_device(
    stream,
    row_tree_nodes,
    input_norm_gain,
    query_key_value_weight,
    adapter_down_weight,
    adapter_up_weight,
    key_value_cache,
    cache_length,
    parents,
    accepted,
    output_weight,
):
    owner_index = lax.axis_index("head")
    feature_rows = query_key_value_weight.shape[0]
    device_width = query_key_value_weight.shape[2]
    adapter_rank_rows = adapter_up_weight.shape[0]
    local_heads = device_width // HEAD_SIZE
    request_count = key_value_cache.shape[1]
    cache_span = key_value_cache.shape[2]
    wide_rows = stream.astype(jnp.float32)
    inverse_rms = lax.rsqrt(jnp.mean(wide_rows * wide_rows, axis=1, keepdims=True) + 1e-05)
    normalized_input = (wide_rows * inverse_rms * input_norm_gain.astype(jnp.float32)).astype(
        jnp.bfloat16
    )
    reduced_rank_rows = jnp.dot(
        normalized_input, adapter_down_weight, preferred_element_type=jnp.float32
    ).astype(jnp.bfloat16)
    feature_block = lax.dynamic_slice_in_dim(
        normalized_input, owner_index * feature_rows, feature_rows, 1
    )
    rank_block = lax.dynamic_slice_in_dim(
        reduced_rank_rows, owner_index * adapter_rank_rows, adapter_rank_rows, 1
    )
    gathered_features, gathered_ranks = (
        lax.all_gather(feature_block, "tok", axis=0, tiled=True),
        lax.all_gather(rank_block, "tok", axis=0, tiled=True),
    )
    projection = query_key_value_weight.reshape(feature_rows, 3 * device_width)
    lifting_matrix = adapter_up_weight.reshape(adapter_rank_rows, 3 * device_width)
    node_to_row = jnp.argsort(row_tree_nodes)
    part_sum = jnp.dot(
        gathered_features[node_to_row], projection, preferred_element_type=jnp.float32
    )
    node_rows = lax.psum_scatter(
        part_sum
        + jnp.dot(gathered_ranks[node_to_row], lifting_matrix, preferred_element_type=jnp.float32),
        "head",
        scatter_dimension=0,
        tiled=True,
    ).astype(jnp.bfloat16)
    triple = node_rows.reshape(request_count, NODES, 3, local_heads, HEAD_SIZE)
    queries = triple[:, :, 0]
    tree_key_rows = triple[:, :, 1]
    tree_value_rows = triple[:, :, 2]
    ancestry = ancestors_of(parents)
    attention_score_scale = HEAD_SIZE ** (-0.5)
    tree_score_matrix = (
        jnp.einsum("rnhd,rmhd->rhnm", queries, tree_key_rows, preferred_element_type=jnp.float32)
        * attention_score_scale
    )
    tree_score_matrix = jnp.where(ancestry[:, None] > 0.5, tree_score_matrix, -jnp.inf)
    keys_cache = key_value_cache[0].reshape(request_count, cache_span, local_heads, HEAD_SIZE)
    values_cache = key_value_cache[1].reshape(request_count, cache_span, local_heads, HEAD_SIZE)
    scores = (
        jnp.einsum("rnhd,rchd->rhnc", queries, keys_cache, preferred_element_type=jnp.float32)
        * attention_score_scale
    )
    positions = lax.broadcasted_iota(jnp.int32, (1, 1, 1, cache_span), 3)
    scores = jnp.where(positions < cache_length[:, None, None, None], scores, -jnp.inf)
    tree_top = jnp.max(tree_score_matrix, axis=-1, keepdims=True)
    largest = jnp.maximum(tree_top, jnp.max(scores, axis=-1, keepdims=True))
    cache_exp = jnp.exp(scores - largest)
    tree_exp = jnp.exp(tree_score_matrix - largest)
    totals = jnp.sum(cache_exp, axis=-1, keepdims=True) + jnp.sum(tree_exp, axis=-1, keepdims=True)
    cache_weights = (cache_exp / totals).astype(jnp.bfloat16)
    tree_weight_matrix = (tree_exp / totals).astype(jnp.bfloat16)
    attention = jnp.einsum(
        "rhnc,rchd->rnhd", cache_weights, values_cache, preferred_element_type=jnp.float32
    )
    attention = attention + jnp.einsum(
        "rhnm,rmhd->rnhd", tree_weight_matrix, tree_value_rows, preferred_element_type=jnp.float32
    )
    head_rows = attention.astype(jnp.bfloat16).reshape(request_count * NODES, device_width)
    node_table = node_rows.reshape(request_count, NODES, 3, device_width)
    chosen = jnp.take_along_axis(node_table, accepted[:, :, None, None], axis=1)
    accepted_kv = jnp.stack([chosen[:, :, 1], chosen[:, :, 2]])
    everything = lax.all_gather(head_rows, "head", axis=0, tiled=True)
    attended = lax.psum_scatter(
        jnp.dot(
            everything[row_tree_nodes], output_weight, preferred_element_type=jnp.float32
        ).astype(jnp.bfloat16),
        "tok",
        scatter_dimension=0,
        tiled=True,
    )
    return (attended, accepted_kv)


def solution(mesh):
    placed = (
        P("tok", None),
        P(),
        P(),
        P("head", None, "tok"),
        P(),
        P("head", None, "tok"),
        P(None, "head", None, "tok"),
        P("head"),
        P("head", None),
        P("head", None),
        P("tok", "head"),
    )
    return jax.shard_map(
        on_device,
        mesh=mesh,
        in_specs=placed,
        out_specs=(P("tok", "head"), P(None, "head", None, "tok")),
        check_vma=False,
    )
```

profile of v0, /device:TPU:0, one launch (start us, length us, event | category | flops | bytes accessed | tf_op | source)
XLA Modules:
  0.0 344.4 jit_solution(10668677327071454545)
XLA Ops:
  7.2 0.0 copy-start
  7.2 0.0 all-gather.3.cloned.1.call-start
  7.2 0.8 convert_element_type.39
  8.1 2.8 fusion
  10.9 3.1 fusion.2
  14.0 0.0 copy-start.2
  14.0 1.8 copy-done.2
  15.8 0.9 constant_dynamic-slice_fusion
  16.7 0.0 all-gather.3.cloned.1.call-update
  16.7 0.0 reduce-scatter.3.cloned.1.call-start
  16.7 4.5 %copy.21 = bf16[448,3,896]{0,2,1:T(8,128)(2,1)} copy(bf16[448,3,896]{2,0,1:T(8,128)(2,1)} %param.14) | data formatting | bytes 4816896 | tf_op args[3]
  21.2 0.0 copy-done.4
  21.2 5.0 %sort.17 = (s32[2048]{0:T(1024)}, s32[2048]{0:T(1024)S(1)}) sort(s32[2048]{0:T(1024)S(1)} %copy-done.4, s32[2048]{0:T(1024)S(1)} %iota.34), dimensions={0}, to_apply=%region_1.0 | sort | flops 22528 | bytes 32768 | tf_op jit(solution)/shard_map/jit(argsort)/sort | solution.py:61
  26.3 3.2 fusion.32
  29.5 0.1 dynamic-slice_convert_fusion
  29.6 15.4 %all_gather.10 = bf16[2048,8]{1,0:T(8,128)(2,1)S(1)} all-gather(bf16[256,8]{1,0:T(8,128)(2,1)S(1)} %dynamic-slice_convert_fusion), channel_id=1, replica_groups=mesh['tok'=8,'head'=16] {'tok'}, dimensions={0}, use_global_device_ids=true | all-gather | bytes 36864 | tf_op jit(solution)/shard_map/all_gather | solution.py:57
  45.0 6.2 %gather_fusion.1 = bf16[2048,8]{1,0:T(8,128)(2,1)S(1)} fusion(bf16[2048,8]{1,0:T(8,128)(2,1)S(1)} %all_gather.10, s32[2048]{0:T(1024)S(1)} %fusion.23), kind=kCustom, calls=%fused_computation.1 | custom fusion | bytes 73728 | tf_op jit(solution)/shard_map/gather | solution.py:67
  51.1 0.0 all-gather.3.cloned.1.call-done
  51.2 11.1 %gather_fusion = bf16[2048,448]{1,0:T(8,128)(2,1)} fusion(bf16[2048,448]{1,0:T(8,128)(2,1)} %all-gather.3.cloned.1.call-done, s32[2048]{0:T(1024)S(1)} %fusion.23), kind=kCustom, calls=%fused_computation | custom fusion | bytes 3678208 | tf_op jit(solution)/shard_map/gather | solution.py:63
  62.3 12.6 %fusion.31 = f32[2048,2688]{1,0:T(8,128)} fusion(bf16[2048,448]{1,0:T(8,128)(2,1)} %gather_fusion, bf16[448,2688]{0,1:T(8,128)(2,1)} %bitcast.63), kind=kOutput, calls=%fused_computation.71 | convolution fusion | flops 4932501504 | bytes 26263552 | tf_op jit(solution)/shard_map/dot_general | solution.py:62
  74.9 14.2 %convolution_add_fusion = f32[2048,2688]{1,0:T(8,128)} fusion(f32[2048,2688]{1,0:T(8,128)} %fusion.31, bf16[2048,8]{1,0:T(8,128)(2,1)S(1)} %gather_fusion.1, bf16[8,2688]{1,0:T(8,128)(2,1)S(1)} %bitcast.65), kind=kOutput, calls=%fused_computation.4 | convolution fusion | flops 93585408 | bytes 44115968 | tf_op jit(solution)/shard_map/dot_general | solution.py:67
  89.1 0.0 reduce-scatter.3.cloned.1.call-update
  89.1 0.2 all-gather.5.cloned.1.call-start
  89.4 0.4 copy-done.5
  89.8 0.3 convolution_minimum_fusion.6
  90.1 0.2 convolution_minimum_fusion.5
  90.3 0.2 convolution_minimum_fusion.4
  90.5 0.2 convolution_minimum_fusion.3
  90.7 0.2 convolution_minimum_fusion.2
  90.9 0.2 convolution_minimum_fusion.1
  91.1 0.2 fusion.11
  91.3 0.1 copy.24
  91.4 10.6 %fusion.28 = (bf16[1,2,2048,896]{3,2,1,0:T(8,128)(2,1)}, bf16[1,2,2048,896]{3,2,1,0:T(8,128)(2,1)}) fusion(bf16[2,2,2048,896]{3,2,1,0:T(8,128)(2,1)} %param.17), kind=kLoop, calls=%fused_computation.68 | loop fusion | bytes 29360128 | tf_op jit(solution)/shard_map/slice | solution.py:83
  102.0 11.3 %copy.23 = bf16[1,2,2048,896]{2,3,1,0:T(8,128)(2,1)} copy(bf16[1,2,2048,896]{3,2,1,0:T(8,128)(2,1)} %get-tuple-element.4) | data formatting | bytes 14680064 | tf_op jit(solution)/shard_map/slice | solution.py:83
  113.3 11.6 %copy.26 = bf16[1,2,2048,896]{2,3,1,0:T(8,128)(2,1)} copy(bf16[1,2,2048,896]{3,2,1,0:T(8,128)(2,1)} %get-tuple-element.5) | data formatting | bytes 14680064 | tf_op jit(solution)/shard_map/slice | solution.py:84
  124.8 0.0 copy-done.7
  124.8 0.1 iota_compare_fusion.3
  124.9 102.2 %reduce-scatter.3.cloned.1.call-done = f32[128,2688]{1,0:T(8,128)} async-done(((f32[2048,2688]{1,0:T(8,128)}), f32[128,2688]{1,0:T(8,128)}) %reduce-scatter.3.cloned.1.call-update) | async-done | bytes 1376272 | tf_op jit(solution)/shard_map/reduce_scatter | solution.py:65
  227.2 1.4 convert_element_type.42
  228.6 0.9 reshape.94
  229.5 0.3 fusion.29
  229.8 0.2 fusion.30
  230.0 0.0 slice-start
  230.0 0.0 slice-start.1
  230.0 4.8 %fusion.3 = (f32[2,4,64]{2,1,0:T(4,128)S(1)}, f32[2,4,64,2048]{3,2,1,0:T(8,128)S(1)}) fusion(pred[2,2048]{1,0:T(4,128)(4,1)S(1)} %iota_compare_fusion.3, bf16[2,2048,4,224]{1,3,2,0:T(8,128)(2,1)} %bitcast.59, bf16[2,64,1,4,224]{4,3,2,1,0:T(4,128)(2,1)S(1)} %get-tuple-element.8), kind=kOutput, calls=%fused_computation.13 | convolution fusion | flops 472907264 | bytes 11769856 | tf_op jit(solution)/shard_map/rnhd,rchd->rhnc/dot_general | solution.py:86
  234.8 0.1 fusion.12
  234.9 1.0 fusion.4
  236.0 2.5 fusion.8
  238.4 0.3 fusion.9
  238.7 0.2 copy.29
  238.9 0.9 reshape.95
  239.8 0.0 all-gather.5.cloned.1.call-update
  239.8 0.0 reduce-scatter.5.cloned.1.call-start
  239.9 0.0 copy-start.8
  239.9 49.4 %all-gather.5.cloned.1.call-done = bf16[2048,896]{1,0:T(8,128)(2,1)} async-done(((bf16[128,896]{1,0:T(8,128)(2,1)}), bf16[2048,896]{1,0:T(8,128)(2,1)}) %all-gather.5.cloned.1.call-update) | async-done | bytes 3670032 | tf_op jit(solution)/shard_map/all_gather | solution.py:108
  289.3 13.1 %gather_fusion.2 = bf16[2048,896]{1,0:T(8,128)(2,1)} fusion(bf16[2048,896]{1,0:T(8,128)(2,1)} %all-gather.5.cloned.1.call-done, s32[2048]{0:T(1024)S(1)} %fusion.24), kind=kCustom, calls=%fused_computation.2 | custom fusion | bytes 7348224 | tf_op jit(solution)/shard_map/gather | solution.py:111
  302.4 4.3 %convolution_convert_fusion = bf16[2048,224]{0,1:T(8,128)(2,1)} fusion(bf16[2048,896]{1,0:T(8,128)(2,1)} %gather_fusion.2, bf16[896,224]{0,1:T(8,128)(2,1)S(1)} %copy-done.8), kind=kOutput, calls=%fused_computation.15 | convolution fusion | flops 822542336 | bytes 4988928 | tf_op jit(solution)/shard_map/dot_general | solution.py:110
  306.7 0.0 reduce-scatter.5.cloned.1.call-update
  306.8 0.1 reshape.122
  306.9 0.2 reshape.96
  307.1 0.7 gather_fusion.3
  307.8 0.1 copy_select_fusion
  307.9 0.6 pad_maximum_fusion
  308.5 29.4 %reduce-scatter.5.cloned.1.call-done = bf16[256,224]{0,1:T(8,128)(2,1)} async-done(((bf16[2048,224]{0,1:T(8,128)(2,1)}), bf16[256,224]{0,1:T(8,128)(2,1)}) %reduce-scatter.5.cloned.1.call-update) | async-done | bytes 114704 | tf_op jit(solution)/shard_map/reduce_scatter | solution.py:109
  (24 shorter events, 0.1 us)
Async XLA Ops:
  7.2 19.1 %copy-start = (bf16[7168,128]{1,0:T(8,128)(2,1)S(1)}, bf16[7168,128]{1,0:T(8,128)(2,1)}, u32[]{:S(2)}) copy-start(bf16[7168,128]{1,0:T(8,128)(2,1)} %param.15) | copy-start | bytes 5505028
  7.2 44.0 %all-gather.3.cloned.1.call-start = ((), (), s32[]{:S(2)}) async-start(), calls=%async_computation.2 | async-start | bytes 2359296 | tf_op jit(solution)/shard_map/all_gather | solution.py:56
  14.0 1.8 copy-start.2
  15.8 5.4 %copy-start.4 = (s32[2048]{0:T(1024)S(1)}, s32[2048]{0:T(1024)}, u32[]{:S(2)}) copy-start(s32[2048]{0:T(1024)} %param.12) | copy-start | bytes 24580
  16.7 210.5 %reduce-scatter.3.cloned.1.call-start = ((), (), s32[]{:S(2)}) async-start(), calls=%async_computation.3 | async-start | bytes 23396352 | tf_op jit(solution)/shard_map/reduce_scatter | solution.py:65
  62.3 12.6 %copy-start.3 = (bf16[8,3,896]{2,0,1:T(8,128)(2,1)S(1)}, bf16[8,3,896]{2,0,1:T(8,128)(2,1)}, u32[]{:S(2)}) copy-start(bf16[8,3,896]{2,0,1:T(8,128)(2,1)} %param.16) | copy-start | bytes 129028
  89.1 0.7 copy-start.5
  89.1 200.1 %all-gather.5.cloned.1.call-start = ((), (), s32[]{:S(2)}) async-start(), calls=%async_computation.4 | async-start | bytes 3899392 | tf_op jit(solution)/shard_map/all_gather | solution.py:108
  113.3 11.6 %copy-start.7 = (s32[2]{0:T(128)S(1)}, s32[2]{0:T(128)}, u32[]{:S(2)}) copy-start(s32[2]{0:T(128)} %param.18) | copy-start | bytes 28
  230.0 6.0 %slice-start = ((s8[7340032]{0:T(1024)(128)(4,1)}), s8[4194304]{0:T(1024)(128)(4,1)S(1)}, s32[]{:S(2)}) async-start(s8[7340032]{0:T(1024)(128)(4,1)} %bitcast.60), calls=%async_computation.6 | async-start | bytes 8388608
  230.0 5.9 %slice-start.1 = ((s8[7340032]{0:T(1024)(128)(4,1)}), s8[3145728]{0:T(1024)(128)(4,1)S(1)}, s32[]{:S(2)}) async-start(s8[7340032]{0:T(1024)(128)(4,1)} %bitcast.60), calls=%async_computation.7 | async-start | bytes 6291456
  239.8 98.1 %reduce-scatter.5.cloned.1.call-start = ((), (), s32[]{:S(2)}) async-start(), calls=%async_computation.5 | async-start | bytes 1032192 | tf_op jit(solution)/shard_map/reduce_scatter | solution.py:109
  239.9 62.5 %copy-start.8 = (bf16[896,224]{0,1:T(8,128)(2,1)S(1)}, bf16[896,224]{0,1:T(8,128)(2,1)}, u32[]{:S(2)}) copy-start(bf16[896,224]{0,1:T(8,128)(2,1)} %param.21) | copy-start | bytes 1204228
  289.3 48.6 %copy-start.1 = (bf16[7168,128]{1,0:T(8,128)(2,1)S(1)}, bf16[7168,128]{1,0:T(8,128)(2,1)}, u32[]{:S(2)}) copy-start(bf16[7168,128]{1,0:T(8,128)(2,1)} %param.15) | copy-start | bytes 5505028
  302.4 4.3 %copy-start.6 = (s32[2,8]{1,0:T(2,128)S(1)}, s32[2,8]{1,0:T(2,128)}, u32[]{:S(2)}) copy-start(s32[2,8]{1,0:T(2,128)} %param.20) | copy-start | bytes 196
Sparse Core Ops, SparseCore 0:
  16.8 28.7 all-gather.2
  89.3 137.8 reduce-scatter.2
  240.0 49.2 all-gather.4
  306.9 31.0 reduce-scatter.4
where the time goes:
time: 345 us; the launch traced here: 344 us
  waiting for transfers between devices  181 us (52%)
  local copies, waits for them, and re-layouts  74.8 us (22%)
  matrix products  43.6 us (13%)
  blocking collectives  15.4 us (4%)
  other arithmetic  15.2 us (4%)
  between operations  14 us (4%)
    reduce_scatter x1, waiting for transfers between devices, on_device(): lax.psum_scatter(part_sum + jnp.dot(gathered_ranks[node_to_row], lifting_...  102 us
    all_gather x1, waiting for transfers between devices, on_device(): everything = lax.all_gather(head_rows, 'head', axis=0, tiled=True)  49.4 us
    reduce_scatter x1, waiting for transfers between devices, on_device(): lax.psum_scatter(jnp.dot(everything[row_tree_nodes], output_weight, prefe...  29.4 us
    slice x2, local copies, waits for them, and re-layouts, on_device(): key_value_cache[0]  21.9 us
    all_gather x1, blocking collectives, on_device(): lax.all_gather(rank_block, 'tok', axis=0, tiled=True)  15.4 us
    dot_general x1, matrix products, on_device(): jnp.dot(gathered_ranks[node_to_row], lifting_matrix, preferred_element_ty...  14.2 us
    gather x1, local copies, waits for them, and re-layouts, on_device(): everything[row_tree_nodes]  13.1 us
    dot_general x1, matrix products, on_device(): jnp.dot(gathered_features[node_to_row], projection, preferred_element_typ...  12.6 us
  transfers between devices with their start and end apart: 4, of which 3 were waited for; matrix products, arithmetic and copies ran while one was open for 16% of the time, Pallas kernels for 0%

commit v1 on v0

v1 whole, which is shorter than its diff:
```python
import functools

import jax
import jax.numpy as jnp
from jax import lax
from jax.experimental import pallas as pl
from jax.experimental.pallas import tpu as pltpu
from jax.sharding import PartitionSpec as P

MESH = pl.DeviceIdType.MESH
F32 = jnp.float32
BF16 = jnp.bfloat16

WIDTH = 7168
COLS = 896
HEAD = 224
LOCAL_HEADS = 4
RANK = 128
NODES = 64
ROWS = 256
KW = 512
UNITS = 12
LAG = 2
PIECE = 512
NEG = float("-inf")
NT = (((1,), (1,)), ((), ()))


def iota(shape, dim):
    return lax.broadcasted_iota(jnp.int32, shape, dim)


def mm(a, b):
    return jnp.dot(a, b, preferred_element_type=F32)


def column_of(row):
    n = row.shape[1]
    eye = iota((n, n), 0) == iota((n, n), 1)
    return jnp.sum(jnp.where(eye, jnp.broadcast_to(row, (n, n)), 0.0), axis=1, keepdims=True)


def row_of(col):
    n = col.shape[0]
    eye = iota((n, n), 0) == iota((n, n), 1)
    return jnp.sum(jnp.where(eye, jnp.broadcast_to(col, (n, n)), 0.0), axis=0, keepdims=True)


def one(mask):
    return jnp.where(mask, 1.0, 0.0).astype(BF16)


def kernel(
    stream_h, nodes, gain, wqkv_h, adown_h, aup, kv_h, clen, parents, accepted, wo_h,
    out_ref, akv_ref,
    stream_v, gain32, adown_v, low_acc, rstd_v, wbuf, kv_v, xbuf, wo_v, part,
    ra, rb, rc, rd, qkv, sort_p, node_q, node_qt, anc_v, qbd, acc_v, m_v, l_v, att, res,
    ld, x_s, x_r, w_s, w_r, rs_s, rs_r, aa_s, aa_r, g1_s, g1_r, g2_s, g2_r, g3_s, g3_r, g4_s, g4_r,
):
    t = lax.axis_index("tok")
    h = lax.axis_index("head")
    z, core = t // 2, t % 2
    y, x = h // 4, h % 4

    def hx(d):
        return y * 4 + (x + d + 4) % 4

    def hy(d):
        return ((y + d + 4) % 4) * 4 + x

    def tz(d, other=False):
        c = 1 - core if other else core
        return ((z + d + 4) % 4) * 2 + c

    xm, xp, x2 = (x + 3) % 4, (x + 1) % 4, (x + 2) % 4
    ym, yp, y2 = (y + 3) % 4, (y + 1) % 4, (y + 2) % 4

    def send(src, dst, ssem, rsem, axis, idx):
        pltpu.make_async_remote_copy(
            src_ref=src, dst_ref=dst, send_sem=ssem, recv_sem=rsem,
            device_id={axis: idx}, device_id_type=MESH,
        ).start()

    def wait(ref, sem):
        pltpu.make_async_copy(ref, ref, sem).wait()

    bar = pltpu.get_barrier_semaphore()
    for d in range(1, 8):
        pl.semaphore_signal(bar, inc=1, device_id={"tok": (t + d) % 8}, device_id_type=MESH)
    for idx in (hx(1), hx(-1), hy(1), hy(-1)):
        pl.semaphore_signal(bar, inc=1, device_id={"head": idx}, device_id_type=MESH)

    loads = []
    for r in range(4):
        c = pltpu.make_async_copy(
            stream_h.at[pl.ds(64 * r, 64)], stream_v.at[pl.ds(64 * r, 64)], ld.at[r]
        )
        c.start()
        loads.append(c)
    adown_c = pltpu.make_async_copy(adown_h, adown_v, ld.at[4])
    adown_c.start()
    odd = h % 2
    koff = pl.multiple_of(64 * odd, 64)
    foff = pl.multiple_of(448 * (1 - odd), 64)
    w_c = pltpu.make_async_copy(wqkv_h, wbuf.at[:, pl.ds(koff, 448), :], ld.at[5])
    w_c.start()
    wo_c = pltpu.make_async_copy(wo_h, wo_v.at[t], ld.at[6])
    wo_c.start()
    kv_c = pltpu.make_async_copy(kv_h, kv_v, ld.at[7])

    mine = nodes[pl.ds(2 * t, 2), :].astype(F32)
    key_row = jnp.concatenate([mine[0:1], mine[1:2]], axis=1)
    key_col = column_of(key_row)
    rank_row = jnp.sum(
        jnp.where(
            jnp.broadcast_to(key_col, (ROWS, ROWS)) < jnp.broadcast_to(key_row, (ROWS, ROWS)), 1.0, 0.0
        ),
        axis=0, keepdims=True,
    )
    sort_p[...] = one(iota((ROWS, ROWS), 0).astype(F32) == jnp.broadcast_to(rank_row, (ROWS, ROWS)))
    gain32[...] = gain[...].astype(F32)
    for p in range(3):
        up = aup[p].astype(F32)
        wbuf[p, pl.ds(foff, 64), :] = jnp.concatenate([up, jnp.zeros((56, COLS), F32)], axis=0).astype(BF16)

    for r in range(4):
        loads[r].wait()

        def sq(kk, acc, r=r):
            blk = stream_v[pl.ds(64 * r, 64), pl.ds(pl.multiple_of(1024 * kk, 1024), 1024)].astype(F32)
            blk = blk * blk
            for b in range(8):
                acc = acc + blk[:, 128 * b:128 * b + 128]
            return acc

        acc = lax.fori_loop(0, 7, sq, jnp.zeros((64, 128), F32))
        mean = jnp.sum(acc, axis=1, keepdims=True) * (1.0 / WIDTH)
        rstd_v[pl.ds(64 * r, 64), :] = jnp.broadcast_to(lax.rsqrt(mean + 1e-5), (64, 128))
    kv_c.start()
    adown_c.wait()
    low_acc[...] = jnp.zeros((ROWS, RANK), F32)

    def normed(block):
        xb = stream_v[:, pl.ds(pl.multiple_of(128 * block, 128), 128)].astype(F32)
        return (xb * rstd_v[...] * gain32[pl.ds(block, 1), :]).astype(BF16)

    def low_step(kk, carry):
        xn = jnp.concatenate([normed(8 * kk + b) for b in range(8)], axis=1)
        low_acc[...] += mm(xn, adown_v[pl.ds(pl.multiple_of(1024 * kk, 1024), 1024), :])
        return carry

    lax.fori_loop(0, 7, low_step, 0)
    first = (7 * h) // 2
    xw = jnp.concatenate([normed(first + b) for b in range(4)], axis=1)
    li = iota((RANK, KW), 1) - foff
    place = one((iota((RANK, KW), 0) - 8 * h == li) & (li >= 0) & (li < 8))
    low = mm(low_acc[...].astype(BF16), place).astype(BF16)
    lane = iota((ROWS, KW), 1) - foff
    xw = jnp.where((lane >= 0) & (lane < 64), low.astype(F32), xw.astype(F32)).astype(BF16)
    xbuf[t] = mm(sort_p[...], xw).astype(BF16)

    pl.semaphore_wait(bar, 11)

    def ag_own(buf, ss, rr):
        own = buf.at[t]
        send(own, own, ss.at[0], rr.at[1], "tok", tz(1))
        send(own, own, ss.at[1], rr.at[2], "tok", tz(-1))
        send(own, own, ss.at[2], rr.at[0], "tok", tz(0, True))

    def ag_near(buf, ss, rr, half):
        a, b = tz(-1), tz(1)
        wait(buf.at[a], rr.at[1])
        piece = buf.at[a, pl.ds(0, half)]
        send(piece, piece, ss.at[3], rr.at[3], "tok", tz(1))
        send(buf.at[a], buf.at[a], ss.at[4], rr.at[4], "tok", tz(0, True))
        wait(buf.at[b], rr.at[2])
        piece = buf.at[b, pl.ds(half, half)]
        send(piece, piece, ss.at[5], rr.at[3], "tok", tz(-1))
        send(buf.at[b], buf.at[b], ss.at[6], rr.at[5], "tok", tz(0, True))

    def ag_far(buf, ss, rr):
        c = tz(2)
        wait(buf.at[c], rr.at[3])
        send(buf.at[c], buf.at[c], ss.at[7], rr.at[6], "tok", tz(0, True))

    def ag_drain(buf, ss, half):
        for i in (0, 1, 2):
            wait(buf.at[t], ss.at[i])
        wait(buf.at[t, pl.ds(0, half)], ss.at[3])
        wait(buf.at[t], ss.at[4])
        wait(buf.at[t, pl.ds(0, half)], ss.at[5])
        wait(buf.at[t], ss.at[6])
        wait(buf.at[t], ss.at[7])

    ag_own(xbuf, x_s, x_r)
    w_c.wait()

    def chip_of(u):
        k = u % 4
        return (z + jnp.where(k == 0, 0, jnp.where(k == 1, 3, jnp.where(k == 2, 1, 2)))) % 4

    def add2(a, b):
        return a.astype(F32) + b.astype(F32)

    def s_matmul(u):
        p, zz = u // 4, chip_of(u)
        for e in range(2):
            prod = mm(xbuf[2 * zz + e], wbuf[p])
            part[u, e] = prod.astype(BF16).reshape(4, 4, 16, COLS)
        ss, rr = rs_s.at[0, u], rs_r.at[0, u]
        send(part.at[u, 0, pl.ds(0, 2), x2], ra.at[u, 0, 0], ss, rr, "head", hx(1))
        send(part.at[u, 0, pl.ds(2, 2), x2], ra.at[u, 0, 1], ss, rr, "head", hx(-1))
        send(part.at[u, 1, y2, pl.ds(0, 2)], ra.at[u, 1, 0], ss, rr, "head", hy(1))
        send(part.at[u, 1, y2, pl.ds(2, 2)], ra.at[u, 1, 1], ss, rr, "head", hy(-1))

    def s_b1(u):
        wait(ra.at[u], rs_r.at[0, u])
        ss, rr = rs_s.at[1, u], rs_r.at[1, u]
        part[u, 0, 0:2, xp] = add2(part[u, 0, 0:2, xp], ra[u, 0, 0]).astype(BF16)
        send(part.at[u, 0, :, xp], rb.at[u, 0, 0], ss, rr, "head", hx(1))
        part[u, 0, 2:4, xm] = add2(part[u, 0, 2:4, xm], ra[u, 0, 1]).astype(BF16)
        send(part.at[u, 0, :, xm], rb.at[u, 0, 1], ss, rr, "head", hx(-1))
        part[u, 1, yp, 0:2] = add2(part[u, 1, yp, 0:2], ra[u, 1, 0]).astype(BF16)
        send(part.at[u, 1, yp], rb.at[u, 1, 0], ss, rr, "head", hy(1))
        part[u, 1, ym, 2:4] = add2(part[u, 1, ym, 2:4], ra[u, 1, 1]).astype(BF16)
        send(part.at[u, 1, ym], rb.at[u, 1, 1], ss, rr, "head", hy(-1))

    def s_a2(u):
        wait(rb.at[u], rs_r.at[1, u])
        ss, rr = rs_s.at[2, u], rs_r.at[2, u]
        part[u, 0, :, x] = (add2(part[u, 0, :, x], rb[u, 0, 0]) + rb[u, 0, 1].astype(F32)).astype(BF16)
        part[u, 1, y] = (add2(part[u, 1, y], rb[u, 1, 0]) + rb[u, 1, 1].astype(F32)).astype(BF16)
        lo, hi = pl.ds(0, 512), pl.ds(512, 384)
        send(part.at[u, 0, y2, x, :, lo], rc.at[u, 0, :, lo], ss, rr, "head", hy(1))
        send(part.at[u, 0, y2, x, :, hi], rc.at[u, 0, :, hi], ss, rr, "head", hy(-1))
        send(part.at[u, 1, y, x2, :, lo], rc.at[u, 1, :, lo], ss, rr, "head", hx(1))
        send(part.at[u, 1, y, x2, :, hi], rc.at[u, 1, :, hi], ss, rr, "head", hx(-1))

    def s_b2(u):
        wait(rc.at[u], rs_r.at[2, u])
        ss, rr = rs_s.at[3, u], rs_r.at[3, u]
        part[u, 0, yp, x, :, 0:512] = add2(part[u, 0, yp, x, :, 0:512], rc[u, 0, :, 0:512]).astype(BF16)
        send(part.at[u, 0, yp, x], rd.at[u, 0, 0], ss, rr, "head", hy(1))
        part[u, 0, ym, x, :, 512:896] = add2(part[u, 0, ym, x, :, 512:896], rc[u, 0, :, 512:896]).astype(BF16)
        send(part.at[u, 0, ym, x], rd.at[u, 0, 1], ss, rr, "head", hy(-1))
        part[u, 1, y, xp, :, 0:512] = add2(part[u, 1, y, xp, :, 0:512], rc[u, 1, :, 0:512]).astype(BF16)
        send(part.at[u, 1, y, xp], rd.at[u, 1, 0], ss, rr, "head", hx(1))
        part[u, 1, y, xm, :, 512:896] = add2(part[u, 1, y, xm, :, 512:896], rc[u, 1, :, 512:896]).astype(BF16)
        send(part.at[u, 1, y, xm], rd.at[u, 1, 1], ss, rr, "head", hx(-1))

    def s_fin(u):
        wait(rd.at[u], rs_r.at[3, u])
        p, zz = u // 4, chip_of(u)
        for e in range(2):
            total = add2(part[u, e, y, x], rd[u, e, 0]) + rd[u, e, 1].astype(F32)
            qkv[p, 2 * zz + e] = total.astype(BF16)

    def prepare():
        node_col = iota((128, 128), 0).astype(F32) + (128 * h).astype(F32)
        acc = jnp.zeros((128, 128), F32)
        for b in range(16):
            line = jnp.broadcast_to(nodes[b:b + 1, :].astype(F32), (128, 128))
            acc = acc + jnp.where(line == node_col, float(b // 2), 0.0)
        tok_col = jnp.sum(acc, axis=1, keepdims=True)
        tok_row = row_of(tok_col)
        before = (jnp.broadcast_to(tok_col, (128, 128)) == jnp.broadcast_to(tok_row, (128, 128))) & (
            iota((128, 128), 1) < iota((128, 128), 0)
        )
        pos_col = 16.0 * tok_col + jnp.sum(jnp.where(before, 1.0, 0.0), axis=1, keepdims=True)
        pos_row = row_of(pos_col)
        node_qt[...] = one(iota((128, 128), 1).astype(F32) == jnp.broadcast_to(pos_col, (128, 128)))
        node_q[...] = one(iota((128, 128), 0).astype(F32) == jnp.broadcast_to(pos_row, (128, 128)))
        for r in range(2):
            par = column_of(parents[r:r + 1, :].astype(F32))
            i0, i1 = iota((NODES, NODES), 0), iota((NODES, NODES), 1)
            anc = one((i0 == i1) | (i1.astype(F32) == jnp.broadcast_to(par, (NODES, NODES))))
            for _ in range(6):
                anc = jnp.minimum(mm(anc, anc), 1.0).astype(BF16)
            anc_v[r] = anc.astype(F32)
        m_v[...] = jnp.full(m_v.shape, NEG, F32)
        l_v[...] = jnp.zeros(l_v.shape, F32)
        acc_v[...] = jnp.zeros(acc_v.shape, F32)

    def in_nodes(p):
        return mm(node_qt[...], qkv[p].reshape(128, COLS))

    def spread_queries():
        q = in_nodes(0)
        head_of = iota((NODES, COLS), 1) // HEAD
        for r in range(2):
            qr = q[NODES * r:NODES * r + NODES]
            for j in range(LOCAL_HEADS):
                qbd[r, NODES * j:NODES * j + NODES, :] = jnp.where(head_of == j, qr, 0.0).astype(BF16)

    scale = HEAD ** -0.5

    def soften(r, s, values):
        m_old = m_v[r]
        m_new = jnp.maximum(m_old, jnp.broadcast_to(jnp.max(s, axis=1, keepdims=True), m_old.shape))
        shrink = jnp.exp(m_old - m_new)
        e = jnp.exp(s - m_new[:, 0:1])
        m_v[r] = m_new
        l_v[r] = l_v[r] * shrink + jnp.broadcast_to(jnp.sum(e, axis=1, keepdims=True), m_old.shape)
        acc_v[r] = acc_v[r] * shrink[:, 0:1] + mm(e.astype(BF16), values)

    def cache_piece(i):
        r, c = i // 4, i % 4
        here = pl.ds(pl.multiple_of(PIECE * c, PIECE), PIECE)
        s = lax.dot_general(qbd[r], kv_v[0, r, here, :], NT, preferred_element_type=F32) * scale
        live = iota((256, PIECE), 1) + PIECE * c < clen[r]
        soften(r, jnp.where(live, s, NEG), kv_v[1, r, here, :])

    last = UNITS + 4 * LAG
    start_att = 4 + 4 * LAG

    def body(it, carry):
        @pl.when(it < UNITS)
        def _():
            @pl.when(it == 0)
            def _():
                wait(xbuf.at[tz(0, True)], x_r.at[0])

            @pl.when(it == 1)
            def _():
                ag_near(xbuf, x_s, x_r, ROWS // 2)
                wait(xbuf.at[tz(-1, True)], x_r.at[4])

            @pl.when(it == 2)
            def _():
                ag_far(xbuf, x_s, x_r)
                wait(xbuf.at[tz(1, True)], x_r.at[5])

            @pl.when(it == 3)
            def _():
                wait(xbuf.at[tz(2, True)], x_r.at[6])

            s_matmul(it)

        for lag, stage in ((LAG, s_b1), (2 * LAG, s_a2), (3 * LAG, s_b2), (4 * LAG, s_fin)):
            @pl.when((it >= lag) & (it < UNITS + lag))
            def _(lag=lag, stage=stage):
                stage(it - lag)

        @pl.when(it == 3)
        def _():
            wo_c.wait()
            ag_own(wo_v, w_s, w_r)

        @pl.when(it == 4)
        def _():
            prepare()

        @pl.when(it == 7)
        def _():
            ag_near(wo_v, w_s, w_r, HEAD // 2)

        @pl.when(it == 9)
        def _():
            ag_far(wo_v, w_s, w_r)

        @pl.when(it == start_att)
        def _():
            kv_c.wait()
            spread_queries()

        @pl.when((it >= start_att) & (it < start_att + 8))
        def _():
            cache_piece(it - start_att)

        return carry

    lax.fori_loop(0, last, body, 0)

    k_n, v_n = in_nodes(1).astype(BF16), in_nodes(2).astype(BF16)
    outs = []
    for r in range(2):
        rows = slice(NODES * r, NODES * r + NODES)
        s = lax.dot_general(qbd[r], k_n[rows], NT, preferred_element_type=F32) * scale
        keep = jnp.concatenate([anc_v[r]] * LOCAL_HEADS, axis=0) > 0.5
        soften(r, jnp.where(keep, s, NEG), v_n[rows])
        norm = acc_v[r] / l_v[r][:, 0:1]
        head_of = iota((NODES, COLS), 1) // HEAD
        o = jnp.zeros((NODES, COLS), F32)
        for j in range(LOCAL_HEADS):
            o = jnp.where(head_of == j, norm[NODES * j:NODES * j + NODES], o)
        outs.append(o.astype(BF16))
    att[...] = mm(node_q[...], jnp.concatenate(outs, axis=0)).astype(BF16).reshape(8, 16, COLS)

    for d in range(1, 8):
        to = (t + d) % 8
        send(att.at[to], res.at[t, h], aa_s.at[d - 1], aa_r.at[d - 1], "tok", to)
    res[t, h] = att[t]
    for r in range(2):
        col = column_of(accepted[r:r + 1, :].astype(F32)) + float(NODES * r)
        pick = one(iota((8, 128), 1).astype(F32) == jnp.broadcast_to(col, (8, 128)))
        akv_ref[0, r] = mm(pick, k_n).astype(BF16)
        akv_ref[1, r] = mm(pick, v_n).astype(BF16)
    for d in range(1, 8):
        wait(res.at[(t - d + 8) % 8, h], aa_r.at[d - 1])

    steps = (0, -1, 1, 2)

    def slot(hf, i, j):
        if hf == 0:
            return ((y + j + 4) % 4) * 4 + (x + i + 4) % 4
        return ((y + i + 4) % 4) * 4 + (x + j + 4) % 4

    def blk(hf, i, j, part_of=None):
        lo, n = (4 * hf, 4) if part_of is None else (4 * hf + 2 * part_of, 2)
        return res.at[pl.ds(lo, n), slot(hf, i, j)]

    def dev(hf, axis, d):
        return slot(hf, d, 0) if axis == 0 else slot(hf, 0, d)

    def first_sends(hf):
        for n, d in enumerate((1, -1)):
            send(blk(hf, 0, 0), blk(hf, 0, 0), g1_s.at[hf, n], g1_r.at[hf, n], "head", dev(hf, 0, d))

    def cross_sends(hf, n_i):
        i = steps[n_i]
        for n, d in enumerate((1, -1)):
            send(blk(hf, i, 0), blk(hf, i, 0), g3_s.at[hf, n_i, n], g3_r.at[hf, n_i, n], "head", dev(hf, 1, d))

    def cross_forward(hf, n_i):
        i = steps[n_i]
        for n, d in enumerate((1, -1)):
            wait(blk(hf, i, -d), g3_r.at[hf, n_i, n])
            send(blk(hf, i, -d, n), blk(hf, i, -d, n), g4_s.at[hf, n_i, n], g4_r.at[hf, n_i], "head", dev(hf, 1, d))

    for hf in range(2):
        first_sends(hf)
    for hf in range(2):
        cross_sends(hf, 0)
    for hf in range(2):
        for n, d in enumerate((1, -1)):
            wait(blk(hf, -d, 0), g1_r.at[hf, n])
            send(blk(hf, -d, 0, n), blk(hf, -d, 0, n), g2_s.at[hf, n], g2_r.at[hf], "head", dev(hf, 0, d))
            cross_sends(hf, 1 + n)
    for hf in range(2):
        cross_forward(hf, 0)
    for hf in range(2):
        wait(blk(hf, 2, 0), g2_r.at[hf])
        cross_sends(hf, 3)
    for n_i in (1, 2, 3):
        for hf in range(2):
            cross_forward(hf, n_i)

    ag_drain(xbuf, x_s, ROWS // 2)
    ag_drain(wo_v, w_s, HEAD // 2)
    for i, c in ((0, tz(0, True)), (4, tz(-1, True)), (5, tz(1, True)), (6, tz(2, True))):
        wait(wo_v.at[c], w_r.at[i])

    def drain(u, carry):
        for k, ref in enumerate((ra, rb, rc, rd)):
            wait(ref.at[u], rs_s.at[k, u])
        return carry

    lax.fori_loop(0, UNITS, drain, 0)
    for hf in range(2):
        for n_i in range(4):
            wait(blk(hf, steps[n_i], 2), g4_r.at[hf, n_i])

    total = jnp.zeros((HEAD, ROWS), F32)
    for s in range(8):
        total = total + lax.dot_general(
            wo_v[s], res[s].reshape(ROWS, COLS), NT, preferred_element_type=F32
        )
    out_ref[...] = mm(total.astype(BF16), sort_p[...]).astype(BF16)

    for d in range(1, 8):
        wait(att.at[0], aa_s.at[d - 1])
    for hf in range(2):
        for n in range(2):
            wait(blk(hf, 0, 0), g1_s.at[hf, n])
            wait(blk(hf, 0, 0, 0), g2_s.at[hf, n])
            for n_i in range(4):
                wait(blk(hf, 0, 0), g3_s.at[hf, n_i, n])
                wait(blk(hf, 0, 0, 0), g4_s.at[hf, n_i, n])


def on_device(stream, row_tree_nodes, gain, wqkv, adown, aup, kv, clen, parents, accepted, wo):
    vm = pl.BlockSpec(memory_space=pltpu.VMEM)
    hbm = pl.BlockSpec(memory_space=pl.ANY)
    sm = pl.BlockSpec(memory_space=pltpu.SMEM)
    dma = pltpu.SemaphoreType.DMA
    v = pltpu.VMEM
    out_t, akv = pl.pallas_call(
        kernel,
        out_shape=(
            jax.ShapeDtypeStruct((HEAD, ROWS), BF16),
            jax.ShapeDtypeStruct((2, 2, 8, COLS), BF16),
        ),
        in_specs=[hbm, vm, vm, hbm, hbm, vm, hbm, sm, vm, vm, hbm],
        out_specs=(vm, vm),
        scratch_shapes=[
            v((ROWS, WIDTH), BF16), v((56, 128), F32), v((WIDTH, RANK), BF16), v((ROWS, RANK), F32),
            v((ROWS, 128), F32), v((3, KW, COLS), BF16), v((2, 2, 2048, COLS), BF16), v((8, ROWS, KW), BF16),
            v((8, HEAD, COLS), BF16), v((UNITS, 2, 4, 4, 16, COLS), BF16),
            v((UNITS, 2, 2, 2, 16, COLS), BF16), v((UNITS, 2, 2, 4, 16, COLS), BF16),
            v((UNITS, 2, 16, COLS), BF16), v((UNITS, 2, 2, 16, COLS), BF16),
            v((3, 8, 16, COLS), BF16), v((ROWS, ROWS), BF16), v((128, 128), BF16), v((128, 128), BF16),
            v((2, NODES, NODES), F32), v((2, 256, COLS), BF16), v((2, 256, COLS), F32),
            v((2, 256, 128), F32), v((2, 256, 128), F32), v((8, 16, COLS), BF16), v((8, 16, 16, COLS), BF16),
            dma((8,)), dma((8,)), dma((7,)), dma((8,)), dma((7,)), dma((4, UNITS)), dma((4, UNITS)),
            dma((7,)), dma((7,)), dma((2, 2)), dma((2, 2)), dma((2, 2)), dma((2,)),
            dma((2, 4, 2)), dma((2, 4, 2)), dma((2, 4, 2)), dma((2, 4)),
        ],
        compiler_params=pltpu.CompilerParams(
            collective_id=0, has_side_effects=True, vmem_limit_bytes=67043328
        ),
        name="tree_verify",
    )(
        stream, row_tree_nodes.reshape(16, 128), gain.reshape(56, 128), jnp.transpose(wqkv, (1, 0, 2)),
        adown, jnp.transpose(aup, (1, 0, 2)), kv, clen, parents, accepted, jnp.transpose(wo),
    )
    return jnp.transpose(out_t), akv


def solution(mesh):
    placed = (
        P("tok", None), P(), P(), P("head", None, "tok"), P(), P("head", None, "tok"),
        P(None, "head", None, "tok"), P("head"), P("head", None), P("head", None), P("tok", "head"),
    )
    return jax.shard_map(
        on_device, mesh=mesh, in_specs=placed,
        out_specs=(P("tok", "head"), P(None, "head", None, "tok")), check_vma=False,
    )
```

time: 345 us -> 120 us (0.35)
  waiting for transfers between devices: 181 us -> 0 us
  Pallas kernels: 0 us -> 117 us
  local copies, waits for them, and re-layouts: 74.8 us -> 3 us
  matrix products: 43.6 us -> 0 us
  blocking collectives: 15.4 us -> 0 us
  other arithmetic: 15.2 us -> 0 us
  between operations: 14 us -> 0.64 us
    reduce_scatter x2 -> x0, waiting for transfers between devices: 132 us -> none  [the longest x1 102 us: on_device(): lax.psum_scatter(part_sum + jnp.dot(gathered_ranks[node_to_row], lifting_...]
    pallas_call x0 -> x1, Pallas kernels: none -> 117 us  [on_device(): pl.pallas_call(kernel, out_shape=(jax.ShapeDtypeStruct((HEAD, ROWS), BF16...]
    all_gather x2 -> x0, waiting for transfers between devices: 49.4 us -> none  [the longest x1 49.4 us: on_device(): everything = lax.all_gather(head_rows, 'head', axis=0, tiled=True)]
    dot_general x15 -> x0, matrix products: 43.6 us -> none  [the longest x1 14.2 us: on_device(): jnp.dot(gathered_ranks[node_to_row], lifting_matrix, preferred_element_ty...]
    slice x4 -> x0, local copies, waits for them, and re-layouts: 33.7 us -> none  [the longest x2 21.9 us: on_device(): key_value_cache[0]]
    gather x5 -> x0, local copies, waits for them, and re-layouts: 31.1 us -> none  [the longest x1 13.1 us: on_device(): everything[row_tree_nodes]]
    all_gather x1 -> x0, blocking collectives: 15.4 us -> none  [on_device(): lax.all_gather(rank_block, 'tok', axis=0, tiled=True)]
    convert_element_type x4 -> x0, other arithmetic: 5.33 us -> none  [the longest x1 3.07 us: on_device(): (wide_rows * inverse_rms * input_norm_gain.astype(jnp.float32)).astype(jn...]
  transfers between devices with their start and end apart: 4 -> 0, of which waited for: 3 -> 0; matrix products, arithmetic and copies ran while one was open for 16% -> 0% of each run, Pallas kernels for 0% -> 0%
where the time goes in v1:
time: 120 us
  Pallas kernels  117 us (98%)
  local copies, waits for them, and re-layouts  3 us (2%)
    pallas_call x1, Pallas kernels, on_device(): pl.pallas_call(kernel, out_shape=(jax.ShapeDtypeStruct((HEAD, ROWS), BF16...  117 us
    unnamed x2, local copies, waits for them, and re-layouts  3 us

profile of v1, /device:TPU:0, one launch (start us, length us, event | category | flops | bytes accessed | tf_op | source)
XLA Modules:
  0.0 120.2 jit_solution(11648515676752938814)
XLA Ops:
  0.6 116.6 %tree_verify.1 = (bf16[224,256]{1,0:T(8,128)(2,1)}, bf16[2,2,8,896]{3,2,1,0:T(8,128)(2,1)}) custom-call(bf16[256,7168]{1,0:T(8,128)(2,1)} %stream_h.1, s32[16,128]{1,0:T(8,128)} %bitcast.11, bf16[56,128]{1,0:T(8,128)(2,1)} %bitcast.10, bf16[3,448,896]{2,1,0:T(8,128)(2,1)} %bitcast.6, bf16[7168,128]{1,0:T(8,128)(2,1)} %adown_h.1, bf16[3,8,896]{2,1,0:T(8,128)(2,1)} %bitcast.9, ...), custom_call_target="tpu_custom_call" | custom-call | tf_op jit(solution)/shard_map/tree_verify/pallas_call | solution.py:487
  117.2 1.6 %copy.15 = bf16[256,224]{0,1:T(8,128)(2,1)} copy(bf16[256,224]{0,1:T(8,128)(2,1)} %bitcast.8) | data formatting | bytes 229376
  118.8 1.4 %copy.16 = bf16[2,2,8,896]{3,2,1,0:T(8,128)(2,1)} copy(bf16[2,2,8,896]{3,2,1,0:T(8,128)(2,1)} %get-tuple-element.9) | data formatting | bytes 114688

commit v2 on v1

--- a/solution.py
+++ b/solution.py
@@ -20,7 +20,9 @@
 ROWS = 256
 KW = 512
 UNITS = 12
-LAG = 2
+LAG = 1
+ASPLIT = 512
+SENT = 464
 PIECE = 512
 NEG = float("-inf")
 NT = (((1,), (1,)), ((), ()))
@@ -53,9 +55,9 @@
 def kernel(
     stream_h, nodes, gain, wqkv_h, adown_h, aup, kv_h, clen, parents, accepted, wo_h,
     out_ref, akv_ref,
-    stream_v, gain32, adown_v, low_acc, rstd_v, wbuf, kv_v, xbuf, wo_v, part,
+    stream_v, gain32, adown_v, low_acc, rstd_v, wbuf, wa, wb, kv_v, xbuf, pack, wo_v, part,
     ra, rb, rc, rd, qkv, sort_p, node_q, node_qt, anc_v, qbd, acc_v, m_v, l_v, att, res,
-    ld, x_s, x_r, w_s, w_r, rs_s, rs_r, aa_s, aa_r, g1_s, g1_r, g2_s, g2_r, g3_s, g3_r, g4_s, g4_r,
+    ld, x_s, x_r, w_s, w_r, p_s, p_r, rs_s, rs_r, aa_s, aa_r, g1_s, g1_r, g2_s, g2_r, g3_s, g3_r, g4_s, g4_r,
 ):
     t = lax.axis_index("tok")
     h = lax.axis_index("head")
@@ -68,12 +70,31 @@
     def hy(d):
         return ((y + d + 4) % 4) * 4 + x
 
+    c1, c2 = jnp.where(core == 0, x, y), jnp.where(core == 0, y, x)
+    par = c2 % 2
+
+    def dev1(d):
+        return jnp.where(core == 0, hx(d), hy(d))
+
+    def dev2(d):
+        return jnp.where(core == 0, hy(d), hx(d))
+
+    dev_a = jnp.where(par == 0, dev2(1), dev2(-1))
+    dev_b = jnp.where(par == 0, dev2(-1), dev2(1))
+
     def tz(d, other=False):
         c = 1 - core if other else core
         return ((z + d + 4) % 4) * 2 + c
 
-    xm, xp, x2 = (x + 3) % 4, (x + 1) % 4, (x + 2) % 4
-    ym, yp, y2 = (y + 3) % 4, (y + 1) % 4, (y + 2) % 4
+    cm, cp, cf = (c1 + 3) % 4, (c1 + 1) % 4, (c1 + 2) % 4
+    own_v = c2 // 2
+    far_v = 1 - own_v
+
+    def slot_of(tok):
+        dz, same = (tok // 2 - z + 4) % 4, tok % 2 == core
+        near = jnp.where(same, 2, 4) + jnp.where(dz == 1, 1, 0)
+        far = jnp.where(same, 6, 7)
+        return jnp.where(dz == 0, tok % 2, jnp.where(dz == 2, far, near))
 
     def send(src, dst, ssem, rsem, axis, idx):
         pltpu.make_async_remote_copy(
@@ -83,12 +104,6 @@
 
     def wait(ref, sem):
         pltpu.make_async_copy(ref, ref, sem).wait()
-
-    bar = pltpu.get_barrier_semaphore()
-    for d in range(1, 8):
-        pl.semaphore_signal(bar, inc=1, device_id={"tok": (t + d) % 8}, device_id_type=MESH)
-    for idx in (hx(1), hx(-1), hy(1), hy(-1)):
-        pl.semaphore_signal(bar, inc=1, device_id={"head": idx}, device_id_type=MESH)
 
     loads = []
     for r in range(4):
@@ -101,7 +116,8 @@
     adown_c.start()
     odd = h % 2
     koff = pl.multiple_of(64 * odd, 64)
-    foff = pl.multiple_of(448 * (1 - odd), 64)
+    foff = pl.multiple_of(448 - 400 * odd, 16)
+    sent = pl.ds(pl.multiple_of(48 * odd, 16), SENT)
     w_c = pltpu.make_async_copy(wqkv_h, wbuf.at[:, pl.ds(koff, 448), :], ld.at[5])
     w_c.start()
     wo_c = pltpu.make_async_copy(wo_h, wo_v.at[t], ld.at[6])
@@ -119,9 +135,20 @@
     )
     sort_p[...] = one(iota((ROWS, ROWS), 0).astype(F32) == jnp.broadcast_to(rank_row, (ROWS, ROWS)))
     gain32[...] = gain[...].astype(F32)
+    blank = jnp.zeros((48, COLS), BF16)
     for p in range(3):
-        up = aup[p].astype(F32)
-        wbuf[p, pl.ds(foff, 64), :] = jnp.concatenate([up, jnp.zeros((56, COLS), F32)], axis=0).astype(BF16)
+        up = jnp.concatenate([aup[p].astype(F32), jnp.zeros((8, COLS), F32)], axis=0).astype(BF16)
+        wbuf[p, pl.ds(pl.multiple_of(464 * (1 - odd), 16), 48), :] = blank
+        wbuf[p, pl.ds(foff, 16), :] = up
+        for lo in (0, 464):
+            wa[p, lo:lo + 48, :] = blank[:, :ASPLIT]
+            wb[p, lo:lo + 48, :] = blank[:, ASPLIT:]
+
+    bar = pltpu.get_barrier_semaphore()
+    for d in range(1, 8):
+        pl.semaphore_signal(bar, inc=1, device_id={"tok": (t + d) % 8}, device_id_type=MESH)
+    for idx in (hx(1), hx(-1), hy(1), hy(-1)):
+        pl.semaphore_signal(bar, inc=1, device_id={"head": idx}, device_id_type=MESH)
 
     for r in range(4):
         loads[r].wait()
@@ -136,30 +163,80 @@
         acc = lax.fori_loop(0, 7, sq, jnp.zeros((64, 128), F32))
         mean = jnp.sum(acc, axis=1, keepdims=True) * (1.0 / WIDTH)
         rstd_v[pl.ds(64 * r, 64), :] = jnp.broadcast_to(lax.rsqrt(mean + 1e-5), (64, 128))
+    pl.semaphore_wait(bar, 11)
+    w_c.wait()
+    for p in range(3):
+        src = wbuf.at[p, sent, pl.ds(0, ASPLIT)]
+        send(src, wa.at[p, sent], p_s.at[p, 0], p_r.at[p, 0], "head", dev_a)
+        src = wbuf.at[p, sent, pl.ds(ASPLIT, COLS - ASPLIT)]
+        send(src, wb.at[p, sent], p_s.at[p, 1], p_r.at[p, 1], "head", dev_b)
     kv_c.start()
     adown_c.wait()
     low_acc[...] = jnp.zeros((ROWS, RANK), F32)
 
-    def normed(block):
-        xb = stream_v[:, pl.ds(pl.multiple_of(128 * block, 128), 128)].astype(F32)
-        return (xb * rstd_v[...] * gain32[pl.ds(block, 1), :]).astype(BF16)
-
     def low_step(kk, carry):
-        xn = jnp.concatenate([normed(8 * kk + b) for b in range(8)], axis=1)
-        low_acc[...] += mm(xn, adown_v[pl.ds(pl.multiple_of(1024 * kk, 1024), 1024), :])
+        parts = []
+        for b in range(8):
+            block = 8 * kk + b
+            here = pl.ds(pl.multiple_of(128 * block, 128), 128)
+            xb = stream_v[:, here].astype(F32)
+            xn = (xb * rstd_v[...] * gain32[pl.ds(block, 1), :]).astype(BF16)
+            stream_v[:, here] = xn
+            parts.append(xn)
+        low_acc[...] += mm(
+            jnp.concatenate(parts, axis=1), adown_v[pl.ds(pl.multiple_of(1024 * kk, 1024), 1024), :]
+        )
         return carry
 
     lax.fori_loop(0, 7, low_step, 0)
-    first = (7 * h) // 2
-    xw = jnp.concatenate([normed(first + b) for b in range(4)], axis=1)
-    li = iota((RANK, KW), 1) - foff
-    place = one((iota((RANK, KW), 0) - 8 * h == li) & (li >= 0) & (li < 8))
-    low = mm(low_acc[...].astype(BF16), place).astype(BF16)
-    lane = iota((ROWS, KW), 1) - foff
-    xw = jnp.where((lane >= 0) & (lane < 64), low.astype(F32), xw.astype(F32)).astype(BF16)
-    xbuf[t] = mm(sort_p[...], xw).astype(BF16)
-
-    pl.semaphore_wait(bar, 11)
+    low = low_acc[...].astype(BF16)
+
+    def window(g):
+        here = pl.ds(pl.multiple_of(128 * ((7 * g) // 2), 128), KW)
+        spot = 448 - 400 * (g % 2)
+        li = iota((RANK, KW), 1) - spot
+        place = one((iota((RANK, KW), 0) - 8 * g == li) & (li >= 0) & (li < 8))
+        terms = mm(low, place)
+        lane = iota((ROWS, KW), 1) - 448 * (1 - g % 2)
+        return jnp.where((lane >= 0) & (lane < 64), terms, stream_v[:, here].astype(F32)).astype(BF16)
+
+    def rows_for(core_to, mine, dst):
+        parity = jnp.where(core_to == 0, y % 2, x % 2)
+        i = iota((128, ROWS), 0)
+        i2, i1 = parity + 2 * (i // 64), (i // 16) % 4
+        rank = 16 * jnp.where(core_to == 0, 4 * i2 + i1, 4 * i1 + i2) + i % 16
+        pick = one(rank.astype(F32) == jnp.broadcast_to(rank_row, (128, ROWS)))
+        step_a = 1 - 2 * parity
+        for n, block in enumerate((None, step_a, -step_a)):
+            if block is None:
+                win = mine
+            else:
+                win = window(jnp.where(core_to == 0, ((y + block + 4) % 4) * 4 + x, y * 4 + (x + block + 4) % 4))
+            dst[:, KW * n:KW * n + KW] = mm(pick, win).astype(BF16)
+
+    mine_win = window(h)
+    rows_for(1 - core, mine_win, pack)
+    send(pack, xbuf.at[0, core], x_s.at[2], x_r.at[0], "tok", tz(0, True))
+    rows_for(core, mine_win, xbuf.at[0, core])
+
+    def x_send(src, to, si, ri, d):
+        send(src, to, x_s.at[si], x_r.at[ri], "tok", tz(d))
+
+    x_send(xbuf.at[0, core], xbuf.at[1, 0], 0, 1, 1)
+    x_send(xbuf.at[0, core], xbuf.at[1, 1], 1, 2, -1)
+
+    def x_mate():
+        got = xbuf.at[0, 1 - core]
+        wait(got, x_r.at[0])
+        x_send(got, xbuf.at[2, 0], 3, 3, 1)
+        x_send(got, xbuf.at[2, 1], 4, 4, -1)
+
+    def x_relay(k):
+        lo, hi = pl.ds(0, 64), pl.ds(64, 64)
+        wait(xbuf.at[k, 0], x_r.at[2 * k - 1])
+        x_send(xbuf.at[k, 0, lo], xbuf.at[3, k - 1, lo], 2 * k + 3, k + 4, 1)
+        wait(xbuf.at[k, 1], x_r.at[2 * k])
+        x_send(xbuf.at[k, 1, hi], xbuf.at[3, k - 1, hi], 2 * k + 4, k + 4, -1)
 
     def ag_own(buf, ss, rr):
         own = buf.at[t]
@@ -192,88 +269,66 @@
         wait(buf.at[t], ss.at[6])
         wait(buf.at[t], ss.at[7])
 
-    ag_own(xbuf, x_s, x_r)
-    w_c.wait()
-
-    def chip_of(u):
-        k = u % 4
-        return (z + jnp.where(k == 0, 0, jnp.where(k == 1, 3, jnp.where(k == 2, 1, 2)))) % 4
-
     def add2(a, b):
         return a.astype(F32) + b.astype(F32)
 
     def s_matmul(u):
-        p, zz = u // 4, chip_of(u)
-        for e in range(2):
-            prod = mm(xbuf[2 * zz + e], wbuf[p])
-            part[u, e] = prod.astype(BF16).reshape(4, 4, 16, COLS)
+        k, p = u // 3, u % 3
+        base = mm(xbuf[k, :, :, 0:KW].reshape(256, KW), wbuf[p])
+        a = base[:, :ASPLIT] + mm(xbuf[k, :, :, KW:2 * KW].reshape(256, KW), wa[p])
+        part[u, :, :, :, :, 0:ASPLIT] = a.astype(BF16).reshape(2, 2, 4, 16, ASPLIT)
+        b = base[:, ASPLIT:] + mm(xbuf[k, :, :, 2 * KW:3 * KW].reshape(256, KW), wb[p])
+        part[u, :, :, :, :, ASPLIT:COLS] = b.astype(BF16).reshape(2, 2, 4, 16, COLS - ASPLIT)
         ss, rr = rs_s.at[0, u], rs_r.at[0, u]
-        send(part.at[u, 0, pl.ds(0, 2), x2], ra.at[u, 0, 0], ss, rr, "head", hx(1))
-        send(part.at[u, 0, pl.ds(2, 2), x2], ra.at[u, 0, 1], ss, rr, "head", hx(-1))
-        send(part.at[u, 1, y2, pl.ds(0, 2)], ra.at[u, 1, 0], ss, rr, "head", hy(1))
-        send(part.at[u, 1, y2, pl.ds(2, 2)], ra.at[u, 1, 1], ss, rr, "head", hy(-1))
+        send(part.at[u, 0, :, cf], ra.at[u, 0], ss, rr, "head", dev1(1))
+        send(part.at[u, 1, :, cf], ra.at[u, 1], ss, rr, "head", dev1(-1))
 
     def s_b1(u):
         wait(ra.at[u], rs_r.at[0, u])
         ss, rr = rs_s.at[1, u], rs_r.at[1, u]
-        part[u, 0, 0:2, xp] = add2(part[u, 0, 0:2, xp], ra[u, 0, 0]).astype(BF16)
-        send(part.at[u, 0, :, xp], rb.at[u, 0, 0], ss, rr, "head", hx(1))
-        part[u, 0, 2:4, xm] = add2(part[u, 0, 2:4, xm], ra[u, 0, 1]).astype(BF16)
-        send(part.at[u, 0, :, xm], rb.at[u, 0, 1], ss, rr, "head", hx(-1))
-        part[u, 1, yp, 0:2] = add2(part[u, 1, yp, 0:2], ra[u, 1, 0]).astype(BF16)
-        send(part.at[u, 1, yp], rb.at[u, 1, 0], ss, rr, "head", hy(1))
-        part[u, 1, ym, 2:4] = add2(part[u, 1, ym, 2:4], ra[u, 1, 1]).astype(BF16)
-        send(part.at[u, 1, ym], rb.at[u, 1, 1], ss, rr, "head", hy(-1))
+        part[u, 0, :, cp] = add2(part[u, 0, :, cp], ra[u, 0]).astype(BF16)
+        send(part.at[u, :, :, cp], rb.at[u, 0], ss, rr, "head", dev1(1))
+        part[u, 1, :, cm] = add2(part[u, 1, :, cm], ra[u, 1]).astype(BF16)
+        send(part.at[u, :, :, cm], rb.at[u, 1], ss, rr, "head", dev1(-1))
 
     def s_a2(u):
         wait(rb.at[u], rs_r.at[1, u])
         ss, rr = rs_s.at[2, u], rs_r.at[2, u]
-        part[u, 0, :, x] = (add2(part[u, 0, :, x], rb[u, 0, 0]) + rb[u, 0, 1].astype(F32)).astype(BF16)
-        part[u, 1, y] = (add2(part[u, 1, y], rb[u, 1, 0]) + rb[u, 1, 1].astype(F32)).astype(BF16)
-        lo, hi = pl.ds(0, 512), pl.ds(512, 384)
-        send(part.at[u, 0, y2, x, :, lo], rc.at[u, 0, :, lo], ss, rr, "head", hy(1))
-        send(part.at[u, 0, y2, x, :, hi], rc.at[u, 0, :, hi], ss, rr, "head", hy(-1))
-        send(part.at[u, 1, y, x2, :, lo], rc.at[u, 1, :, lo], ss, rr, "head", hx(1))
-        send(part.at[u, 1, y, x2, :, hi], rc.at[u, 1, :, hi], ss, rr, "head", hx(-1))
+        part[u, :, :, c1] = (add2(part[u, :, :, c1], rb[u, 0]) + rb[u, 1].astype(F32)).astype(BF16)
+        send(part.at[u, 0, far_v, c1], rc.at[u, 0], ss, rr, "head", dev2(1))
+        send(part.at[u, 1, far_v, c1], rc.at[u, 1], ss, rr, "head", dev2(-1))
 
     def s_b2(u):
         wait(rc.at[u], rs_r.at[2, u])
         ss, rr = rs_s.at[3, u], rs_r.at[3, u]
-        part[u, 0, yp, x, :, 0:512] = add2(part[u, 0, yp, x, :, 0:512], rc[u, 0, :, 0:512]).astype(BF16)
-        send(part.at[u, 0, yp, x], rd.at[u, 0, 0], ss, rr, "head", hy(1))
-        part[u, 0, ym, x, :, 512:896] = add2(part[u, 0, ym, x, :, 512:896], rc[u, 0, :, 512:896]).astype(BF16)
-        send(part.at[u, 0, ym, x], rd.at[u, 0, 1], ss, rr, "head", hy(-1))
-        part[u, 1, y, xp, :, 0:512] = add2(part[u, 1, y, xp, :, 0:512], rc[u, 1, :, 0:512]).astype(BF16)
-        send(part.at[u, 1, y, xp], rd.at[u, 1, 0], ss, rr, "head", hx(1))
-        part[u, 1, y, xm, :, 512:896] = add2(part[u, 1, y, xm, :, 512:896], rc[u, 1, :, 512:896]).astype(BF16)
-        send(part.at[u, 1, y, xm], rd.at[u, 1, 1], ss, rr, "head", hx(-1))
+        send(rc.at[u, 0], rd.at[u, 0], ss, rr, "head", dev2(1))
+        send(rc.at[u, 1], rd.at[u, 1], ss, rr, "head", dev2(-1))
 
     def s_fin(u):
         wait(rd.at[u], rs_r.at[3, u])
-        p, zz = u // 4, chip_of(u)
+        k, p = u // 3, u % 3
         for e in range(2):
-            total = add2(part[u, e, y, x], rd[u, e, 0]) + rd[u, e, 1].astype(F32)
-            qkv[p, 2 * zz + e] = total.astype(BF16)
+            qkv[p, 2 * k + e] = add2(part[u, e, own_v, c1], rd[u, e]).astype(BF16)
 
     def prepare():
         node_col = iota((128, 128), 0).astype(F32) + (128 * h).astype(F32)
         acc = jnp.zeros((128, 128), F32)
         for b in range(16):
             line = jnp.broadcast_to(nodes[b:b + 1, :].astype(F32), (128, 128))
-            acc = acc + jnp.where(line == node_col, float(b // 2), 0.0)
-        tok_col = jnp.sum(acc, axis=1, keepdims=True)
-        tok_row = row_of(tok_col)
-        before = (jnp.broadcast_to(tok_col, (128, 128)) == jnp.broadcast_to(tok_row, (128, 128))) & (
+            acc = acc + jnp.where(line == node_col, slot_of(b // 2).astype(F32), 0.0)
+        slot_col = jnp.sum(acc, axis=1, keepdims=True)
+        slot_row = row_of(slot_col)
+        before = (jnp.broadcast_to(slot_col, (128, 128)) == jnp.broadcast_to(slot_row, (128, 128))) & (
             iota((128, 128), 1) < iota((128, 128), 0)
         )
-        pos_col = 16.0 * tok_col + jnp.sum(jnp.where(before, 1.0, 0.0), axis=1, keepdims=True)
+        pos_col = 16.0 * slot_col + jnp.sum(jnp.where(before, 1.0, 0.0), axis=1, keepdims=True)
         pos_row = row_of(pos_col)
         node_qt[...] = one(iota((128, 128), 1).astype(F32) == jnp.broadcast_to(pos_col, (128, 128)))
         node_q[...] = one(iota((128, 128), 0).astype(F32) == jnp.broadcast_to(pos_row, (128, 128)))
         for r in range(2):
-            par = column_of(parents[r:r + 1, :].astype(F32))
+            up = column_of(parents[r:r + 1, :].astype(F32))
             i0, i1 = iota((NODES, NODES), 0), iota((NODES, NODES), 1)
-            anc = one((i0 == i1) | (i1.astype(F32) == jnp.broadcast_to(par, (NODES, NODES))))
+            anc = one((i0 == i1) | (i1.astype(F32) == jnp.broadcast_to(up, (NODES, NODES))))
             for _ in range(6):
                 anc = jnp.minimum(mm(anc, anc), 1.0).astype(BF16)
             anc_v[r] = anc.astype(F32)
@@ -310,51 +365,55 @@
         live = iota((256, PIECE), 1) + PIECE * c < clen[r]
         soften(r, jnp.where(live, s, NEG), kv_v[1, r, here, :])
 
-    last = UNITS + 4 * LAG
-    start_att = 4 + 4 * LAG
+    start_att = 9 + 4 * LAG
+    last = start_att + 8
 
     def body(it, carry):
-        @pl.when(it < UNITS)
-        def _():
-            @pl.when(it == 0)
-            def _():
-                wait(xbuf.at[tz(0, True)], x_r.at[0])
-
-            @pl.when(it == 1)
-            def _():
-                ag_near(xbuf, x_s, x_r, ROWS // 2)
-                wait(xbuf.at[tz(-1, True)], x_r.at[4])
-
-            @pl.when(it == 2)
-            def _():
-                ag_far(xbuf, x_s, x_r)
-                wait(xbuf.at[tz(1, True)], x_r.at[5])
-
-            @pl.when(it == 3)
-            def _():
-                wait(xbuf.at[tz(2, True)], x_r.at[6])
-
-            s_matmul(it)
-
-        for lag, stage in ((LAG, s_b1), (2 * LAG, s_a2), (3 * LAG, s_b2), (4 * LAG, s_fin)):
+        for lag, stage in ((4 * LAG, s_fin), (3 * LAG, s_b2), (2 * LAG, s_a2), (LAG, s_b1)):
             @pl.when((it >= lag) & (it < UNITS + lag))
             def _(lag=lag, stage=stage):
                 stage(it - lag)
 
-        @pl.when(it == 3)
+        @pl.when(it < UNITS)
+        def _():
+            @pl.when(it < 3)
+            def _():
+                wait(wa.at[it, sent], p_r.at[it, 0])
+                wait(wb.at[it, sent], p_r.at[it, 1])
+
+            @pl.when(it == 0)
+            def _():
+                x_mate()
+
+            @pl.when(it == 3)
+            def _():
+                x_relay(1)
+
+            @pl.when(it == 6)
+            def _():
+                x_relay(2)
+
+            @pl.when(it == 9)
+            def _():
+                wait(xbuf.at[3, 0], x_r.at[5])
+                wait(xbuf.at[3, 1], x_r.at[6])
+
+            s_matmul(it)
+
+        @pl.when(it == 1)
+        def _():
+            prepare()
+
+        @pl.when(it == 6)
         def _():
             wo_c.wait()
             ag_own(wo_v, w_s, w_r)
 
-        @pl.when(it == 4)
-        def _():
-            prepare()
-
-        @pl.when(it == 7)
+        @pl.when(it == 11)
         def _():
             ag_near(wo_v, w_s, w_r, HEAD // 2)
 
-        @pl.when(it == 9)
+        @pl.when(it == start_att + 5)
         def _():
             ag_far(wo_v, w_s, w_r)
 
@@ -370,6 +429,27 @@
         return carry
 
     lax.fori_loop(0, last, body, 0)
+
+    def drain_rs():
+        for i in (0, 1, 3, 4):
+            wait(xbuf.at[0, 0], x_s.at[i])
+        wait(pack, x_s.at[2])
+        for i in (5, 6, 7, 8):
+            wait(xbuf.at[0, 0, pl.ds(0, 64)], x_s.at[i])
+        ag_drain(wo_v, w_s, HEAD // 2)
+        for i, c in ((0, tz(0, True)), (4, tz(-1, True)), (5, tz(1, True)), (6, tz(2, True))):
+            wait(wo_v.at[c], w_r.at[i])
+        for p in range(3):
+            wait(wa.at[p, sent], p_s.at[p, 0])
+            wait(wb.at[p, sent], p_s.at[p, 1])
+
+        def drain(u, carry):
+            for k, ref in enumerate((ra, rb, rc, rd)):
+                wait(ref.at[u], rs_s.at[k, u])
+            return carry
+
+        lax.fori_loop(0, UNITS, drain, 0)
+
 
     k_n, v_n = in_nodes(1).astype(BF16), in_nodes(2).astype(BF16)
     outs = []
@@ -388,8 +468,8 @@
 
     for d in range(1, 8):
         to = (t + d) % 8
-        send(att.at[to], res.at[t, h], aa_s.at[d - 1], aa_r.at[d - 1], "tok", to)
-    res[t, h] = att[t]
+        send(att.at[slot_of(to)], res.at[t, h], aa_s.at[d - 1], aa_r.at[d - 1], "tok", to)
+    res[t, h] = att[core]
     for r in range(2):
         col = column_of(accepted[r:r + 1, :].astype(F32)) + float(NODES * r)
         pick = one(iota((8, 128), 1).astype(F32) == jnp.broadcast_to(col, (8, 128)))
@@ -397,6 +477,7 @@
         akv_ref[1, r] = mm(pick, v_n).astype(BF16)
     for d in range(1, 8):
         wait(res.at[(t - d + 8) % 8, h], aa_r.at[d - 1])
+
 
     steps = (0, -1, 1, 2)
 
@@ -445,17 +526,7 @@
         for hf in range(2):
             cross_forward(hf, n_i)
 
-    ag_drain(xbuf, x_s, ROWS // 2)
-    ag_drain(wo_v, w_s, HEAD // 2)
-    for i, c in ((0, tz(0, True)), (4, tz(-1, True)), (5, tz(1, True)), (6, tz(2, True))):
-        wait(wo_v.at[c], w_r.at[i])
-
-    def drain(u, carry):
-        for k, ref in enumerate((ra, rb, rc, rd)):
-            wait(ref.at[u], rs_s.at[k, u])
-        return carry
-
-    lax.fori_loop(0, UNITS, drain, 0)
+    drain_rs()
     for hf in range(2):
         for n_i in range(4):
             wait(blk(hf, steps[n_i], 2), g4_r.at[hf, n_i])
@@ -494,14 +565,16 @@
         out_specs=(vm, vm),
         scratch_shapes=[
             v((ROWS, WIDTH), BF16), v((56, 128), F32), v((WIDTH, RANK), BF16), v((ROWS, RANK), F32),
-            v((ROWS, 128), F32), v((3, KW, COLS), BF16), v((2, 2, 2048, COLS), BF16), v((8, ROWS, KW), BF16),
-            v((8, HEAD, COLS), BF16), v((UNITS, 2, 4, 4, 16, COLS), BF16),
-            v((UNITS, 2, 2, 2, 16, COLS), BF16), v((UNITS, 2, 2, 4, 16, COLS), BF16),
-            v((UNITS, 2, 16, COLS), BF16), v((UNITS, 2, 2, 16, COLS), BF16),
+            v((ROWS, 128), F32), v((3, KW, COLS), BF16), v((3, KW, ASPLIT), BF16),
+            v((3, KW, COLS - ASPLIT), BF16), v((2, 2, 2048, COLS), BF16), v((4, 2, 128, 3 * KW), BF16),
+            v((128, 3 * KW), BF16),
+            v((8, HEAD, COLS), BF16), v((UNITS, 2, 2, 4, 16, COLS), BF16),
+            v((UNITS, 2, 2, 16, COLS), BF16), v((UNITS, 2, 2, 2, 16, COLS), BF16),
+            v((UNITS, 2, 16, COLS), BF16), v((UNITS, 2, 16, COLS), BF16),
             v((3, 8, 16, COLS), BF16), v((ROWS, ROWS), BF16), v((128, 128), BF16), v((128, 128), BF16),
             v((2, NODES, NODES), F32), v((2, 256, COLS), BF16), v((2, 256, COLS), F32),
             v((2, 256, 128), F32), v((2, 256, 128), F32), v((8, 16, COLS), BF16), v((8, 16, 16, COLS), BF16),
-            dma((8,)), dma((8,)), dma((7,)), dma((8,)), dma((7,)), dma((4, UNITS)), dma((4, UNITS)),
+            dma((8,)), dma((9,)), dma((7,)), dma((8,)), dma((7,)), dma((3, 2)), dma((3, 2)), dma((4, UNITS)), dma((4, UNITS)),
             dma((7,)), dma((7,)), dma((2, 2)), dma((2, 2)), dma((2, 2)), dma((2,)),
             dma((2, 4, 2)), dma((2, 4, 2)), dma((2, 4, 2)), dma((2, 4)),
         ],

time: 120 us -> 138 us (1.15)
  Pallas kernels: 117 us -> 134 us
    pallas_call x1, Pallas kernels: 117 us -> 134 us  [on_device(): pl.pallas_call(kernel, out_shape=(jax.ShapeDtypeStruct((HEAD, ROWS), BF16...]
where the time goes in v2:
time: 138 us
  Pallas kernels  134 us (97%)
  local copies, waits for them, and re-layouts  3 us (2%)
    pallas_call x1, Pallas kernels, on_device(): pl.pallas_call(kernel, out_shape=(jax.ShapeDtypeStruct((HEAD, ROWS), BF16...  134 us
    unnamed x2, local copies, waits for them, and re-layouts  3 us

profile of v2, /device:TPU:0, one launch (start us, length us, event | category | flops | bytes accessed | tf_op | source)
XLA Modules:
  0.0 137.9 jit_solution(5709814421278419593)
XLA Ops:
  0.6 134.2 %tree_verify.1 = (bf16[224,256]{1,0:T(8,128)(2,1)}, bf16[2,2,8,896]{3,2,1,0:T(8,128)(2,1)}) custom-call(bf16[256,7168]{1,0:T(8,128)(2,1)} %stream_h.1, s32[16,128]{1,0:T(8,128)} %bitcast.11, bf16[56,128]{1,0:T(8,128)(2,1)} %bitcast.10, bf16[3,448,896]{2,1,0:T(8,128)(2,1)} %bitcast.6, bf16[7168,128]{1,0:T(8,128)(2,1)} %adown_h.1, bf16[3,8,896]{2,1,0:T(8,128)(2,1)} %bitcast.9, ...), custom_call_target="tpu_custom_call" | custom-call | tf_op jit(solution)/shard_map/tree_verify/pallas_call | solution.py:558
  134.9 1.6 %copy.15 = bf16[256,224]{0,1:T(8,128)(2,1)} copy(bf16[256,224]{0,1:T(8,128)(2,1)} %bitcast.8) | data formatting | bytes 229376
  136.4 1.4 %copy.16 = bf16[2,2,8,896]{3,2,1,0:T(8,128)(2,1)} copy(bf16[2,2,8,896]{3,2,1,0:T(8,128)(2,1)} %get-tuple-element.9) | data formatting | bytes 114688

commit v3 on v2

--- a/solution.py
+++ b/solution.py
@@ -20,7 +20,7 @@
 ROWS = 256
 KW = 512
 UNITS = 12
-LAG = 1
+LAG = 3
 ASPLIT = 512
 SENT = 464
 PIECE = 512
@@ -56,7 +56,7 @@
     stream_h, nodes, gain, wqkv_h, adown_h, aup, kv_h, clen, parents, accepted, wo_h,
     out_ref, akv_ref,
     stream_v, gain32, adown_v, low_acc, rstd_v, wbuf, wa, wb, kv_v, xbuf, pack, wo_v, part,
-    ra, rb, rc, rd, qkv, sort_p, node_q, node_qt, anc_v, qbd, acc_v, m_v, l_v, att, res,
+    ra, rb, mine_sum, qkv, sort_p, node_q, node_qt, anc_v, qbd, acc_v, m_v, l_v, att, res,
     ld, x_s, x_r, w_s, w_r, p_s, p_r, rs_s, rs_r, aa_s, aa_r, g1_s, g1_r, g2_s, g2_r, g3_s, g3_r, g4_s, g4_r,
 ):
     t = lax.axis_index("tok")
@@ -105,6 +105,12 @@
     def wait(ref, sem):
         pltpu.make_async_copy(ref, ref, sem).wait()
 
+    odd = h % 2
+    koff = pl.multiple_of(64 * odd, 64)
+    foff = pl.multiple_of(448 - 400 * odd, 16)
+    sent = pl.ds(pl.multiple_of(48 * odd, 16), SENT)
+    w_c = pltpu.make_async_copy(wqkv_h, wbuf.at[:, pl.ds(koff, 448), :], ld.at[5])
+    w_c.start()
     loads = []
     for r in range(4):
         c = pltpu.make_async_copy(
@@ -114,15 +120,26 @@
         loads.append(c)
     adown_c = pltpu.make_async_copy(adown_h, adown_v, ld.at[4])
     adown_c.start()
-    odd = h % 2
-    koff = pl.multiple_of(64 * odd, 64)
-    foff = pl.multiple_of(448 - 400 * odd, 16)
-    sent = pl.ds(pl.multiple_of(48 * odd, 16), SENT)
-    w_c = pltpu.make_async_copy(wqkv_h, wbuf.at[:, pl.ds(koff, 448), :], ld.at[5])
-    w_c.start()
     wo_c = pltpu.make_async_copy(wo_h, wo_v.at[t], ld.at[6])
     wo_c.start()
     kv_c = pltpu.make_async_copy(kv_h, kv_v, ld.at[7])
+
+    blank = jnp.zeros((48, COLS), BF16)
+    for p in range(3):
+        for lo in (0, 464):
+            wa[p, lo:lo + 48, :] = blank[:, :ASPLIT]
+            wb[p, lo:lo + 48, :] = blank[:, ASPLIT:]
+
+    bar = pltpu.get_barrier_semaphore()
+    for d in range(1, 8):
+        pl.semaphore_signal(bar, inc=1, device_id={"tok": (t + d) % 8}, device_id_type=MESH)
+    for idx in (hx(1), hx(-1), hx(2), hy(1), hy(-1), hy(2)):
+        pl.semaphore_signal(bar, inc=1, device_id={"head": idx}, device_id_type=MESH)
+
+    for p in range(3):
+        up = jnp.concatenate([aup[p].astype(F32), jnp.zeros((8, COLS), F32)], axis=0).astype(BF16)
+        wbuf[p, pl.ds(pl.multiple_of(464 * (1 - odd), 16), 48), :] = blank
+        wbuf[p, pl.ds(foff, 16), :] = up
 
     mine = nodes[pl.ds(2 * t, 2), :].astype(F32)
     key_row = jnp.concatenate([mine[0:1], mine[1:2]], axis=1)
@@ -135,20 +152,17 @@
     )
     sort_p[...] = one(iota((ROWS, ROWS), 0).astype(F32) == jnp.broadcast_to(rank_row, (ROWS, ROWS)))
     gain32[...] = gain[...].astype(F32)
-    blank = jnp.zeros((48, COLS), BF16)
-    for p in range(3):
-        up = jnp.concatenate([aup[p].astype(F32), jnp.zeros((8, COLS), F32)], axis=0).astype(BF16)
-        wbuf[p, pl.ds(pl.multiple_of(464 * (1 - odd), 16), 48), :] = blank
-        wbuf[p, pl.ds(foff, 16), :] = up
-        for lo in (0, 464):
-            wa[p, lo:lo + 48, :] = blank[:, :ASPLIT]
-            wb[p, lo:lo + 48, :] = blank[:, ASPLIT:]
-
-    bar = pltpu.get_barrier_semaphore()
-    for d in range(1, 8):
-        pl.semaphore_signal(bar, inc=1, device_id={"tok": (t + d) % 8}, device_id_type=MESH)
-    for idx in (hx(1), hx(-1), hy(1), hy(-1)):
-        pl.semaphore_signal(bar, inc=1, device_id={"head": idx}, device_id_type=MESH)
+
+    def finish_cut():
+        for c in (wo_c, kv_c):
+            c.wait()
+        for p in range(3):
+            wait(wa.at[p, sent], p_r.at[p, 0])
+            wait(wb.at[p, sent], p_r.at[p, 1])
+            wait(wa.at[p, sent], p_s.at[p, 0])
+            wait(wb.at[p, sent], p_s.at[p, 1])
+        out_ref[...] = jnp.zeros(out_ref.shape, BF16)
+        akv_ref[...] = jnp.zeros(akv_ref.shape, BF16)
 
     for r in range(4):
         loads[r].wait()
@@ -163,13 +177,14 @@
         acc = lax.fori_loop(0, 7, sq, jnp.zeros((64, 128), F32))
         mean = jnp.sum(acc, axis=1, keepdims=True) * (1.0 / WIDTH)
         rstd_v[pl.ds(64 * r, 64), :] = jnp.broadcast_to(lax.rsqrt(mean + 1e-5), (64, 128))
-    pl.semaphore_wait(bar, 11)
+    pl.semaphore_wait(bar, 13)
     w_c.wait()
     for p in range(3):
         src = wbuf.at[p, sent, pl.ds(0, ASPLIT)]
         send(src, wa.at[p, sent], p_s.at[p, 0], p_r.at[p, 0], "head", dev_a)
         src = wbuf.at[p, sent, pl.ds(ASPLIT, COLS - ASPLIT)]
         send(src, wb.at[p, sent], p_s.at[p, 1], p_r.at[p, 1], "head", dev_b)
+
     kv_c.start()
     adown_c.wait()
     low_acc[...] = jnp.zeros((ROWS, RANK), F32)
@@ -215,15 +230,14 @@
             dst[:, KW * n:KW * n + KW] = mm(pick, win).astype(BF16)
 
     mine_win = window(h)
+    def x_send(src, to, si, ri, d):
+        send(src, to, x_s.at[si], x_r.at[ri], "tok", tz(d))
+
+    rows_for(core, mine_win, xbuf.at[0, core])
+    x_send(xbuf.at[0, core], xbuf.at[1, 0], 0, 1, 1)
+    x_send(xbuf.at[0, core], xbuf.at[1, 1], 1, 2, -1)
     rows_for(1 - core, mine_win, pack)
     send(pack, xbuf.at[0, core], x_s.at[2], x_r.at[0], "tok", tz(0, True))
-    rows_for(core, mine_win, xbuf.at[0, core])
-
-    def x_send(src, to, si, ri, d):
-        send(src, to, x_s.at[si], x_r.at[ri], "tok", tz(d))
-
-    x_send(xbuf.at[0, core], xbuf.at[1, 0], 0, 1, 1)
-    x_send(xbuf.at[0, core], xbuf.at[1, 1], 1, 2, -1)
 
     def x_mate():
         got = xbuf.at[0, 1 - core]
@@ -233,41 +247,28 @@
 
     def x_relay(k):
         lo, hi = pl.ds(0, 64), pl.ds(64, 64)
-        wait(xbuf.at[k, 0], x_r.at[2 * k - 1])
-        x_send(xbuf.at[k, 0, lo], xbuf.at[3, k - 1, lo], 2 * k + 3, k + 4, 1)
-        wait(xbuf.at[k, 1], x_r.at[2 * k])
-        x_send(xbuf.at[k, 1, hi], xbuf.at[3, k - 1, hi], 2 * k + 4, k + 4, -1)
-
-    def ag_own(buf, ss, rr):
-        own = buf.at[t]
-        send(own, own, ss.at[0], rr.at[1], "tok", tz(1))
-        send(own, own, ss.at[1], rr.at[2], "tok", tz(-1))
-        send(own, own, ss.at[2], rr.at[0], "tok", tz(0, True))
-
-    def ag_near(buf, ss, rr, half):
-        a, b = tz(-1), tz(1)
-        wait(buf.at[a], rr.at[1])
-        piece = buf.at[a, pl.ds(0, half)]
-        send(piece, piece, ss.at[3], rr.at[3], "tok", tz(1))
-        send(buf.at[a], buf.at[a], ss.at[4], rr.at[4], "tok", tz(0, True))
-        wait(buf.at[b], rr.at[2])
-        piece = buf.at[b, pl.ds(half, half)]
-        send(piece, piece, ss.at[5], rr.at[3], "tok", tz(-1))
-        send(buf.at[b], buf.at[b], ss.at[6], rr.at[5], "tok", tz(0, True))
-
-    def ag_far(buf, ss, rr):
-        c = tz(2)
-        wait(buf.at[c], rr.at[3])
-        send(buf.at[c], buf.at[c], ss.at[7], rr.at[6], "tok", tz(0, True))
-
-    def ag_drain(buf, ss, half):
-        for i in (0, 1, 2):
-            wait(buf.at[t], ss.at[i])
-        wait(buf.at[t, pl.ds(0, half)], ss.at[3])
-        wait(buf.at[t], ss.at[4])
-        wait(buf.at[t, pl.ds(0, half)], ss.at[5])
-        wait(buf.at[t], ss.at[6])
-        wait(buf.at[t], ss.at[7])
+        x_send(xbuf.at[k, 0, lo], xbuf.at[3, k - 1, lo], 3 + 2 * k, k + 4, 1)
+        x_send(xbuf.at[k, 1, hi], xbuf.at[3, k - 1, hi], 4 + 2 * k, k + 4, -1)
+
+    near = tuple((d, tz(d)) for d in (-1, 1, 2))
+
+    def wo_own():
+        own = wo_v.at[t]
+        send(own, own, w_s.at[0], w_r.at[0], "tok", tz(0, True))
+        for n, d in enumerate((1, -1, 2)):
+            send(own, own, w_s.at[1 + n], w_r.at[1 + n], "tok", tz(d))
+
+    def wo_mate():
+        for n, (d, src) in enumerate(near):
+            wait(wo_v.at[src], w_r.at[1 + n])
+            send(wo_v.at[src], wo_v.at[src], w_s.at[4 + n], w_r.at[4 + n], "tok", tz(0, True))
+
+    def wo_rest():
+        wait(wo_v.at[t], w_r.at[0])
+        for n in range(3):
+            wait(wo_v.at[t], w_r.at[4 + n])
+        for n in range(7):
+            wait(wo_v.at[t], w_s.at[n])
 
     def add2(a, b):
         return a.astype(F32) + b.astype(F32)
@@ -279,36 +280,39 @@
         part[u, :, :, :, :, 0:ASPLIT] = a.astype(BF16).reshape(2, 2, 4, 16, ASPLIT)
         b = base[:, ASPLIT:] + mm(xbuf[k, :, :, 2 * KW:3 * KW].reshape(256, KW), wb[p])
         part[u, :, :, :, :, ASPLIT:COLS] = b.astype(BF16).reshape(2, 2, 4, 16, COLS - ASPLIT)
+        s_a1(u)
+
+    def s_a1(u):
         ss, rr = rs_s.at[0, u], rs_r.at[0, u]
-        send(part.at[u, 0, :, cf], ra.at[u, 0], ss, rr, "head", dev1(1))
-        send(part.at[u, 1, :, cf], ra.at[u, 1], ss, rr, "head", dev1(-1))
+        send(part.at[u, 0, :, cf], ra.at[u, 2, 0], ss, rr, "head", dev1(1))
+        send(part.at[u, 1, :, cf], ra.at[u, 2, 1], ss, rr, "head", dev1(-1))
 
     def s_b1(u):
-        wait(ra.at[u], rs_r.at[0, u])
+        wait(ra.at[u, 2], rs_r.at[0, u])
+        ss, rr = rs_s.at[2, u], rs_r.at[2, u]
+        part[u, 0, :, cp] = add2(part[u, 0, :, cp], ra[u, 2, 0]).astype(BF16)
+        send(part.at[u, :, :, cp], ra.at[u, 0], ss, rr, "head", dev1(1))
+        part[u, 1, :, cm] = add2(part[u, 1, :, cm], ra[u, 2, 1]).astype(BF16)
+        send(part.at[u, :, :, cm], ra.at[u, 1], ss, rr, "head", dev1(-1))
+
+    def s_sum(u):
+        wait(ra.at[u, 0:2], rs_r.at[2, u])
         ss, rr = rs_s.at[1, u], rs_r.at[1, u]
-        part[u, 0, :, cp] = add2(part[u, 0, :, cp], ra[u, 0]).astype(BF16)
-        send(part.at[u, :, :, cp], rb.at[u, 0], ss, rr, "head", dev1(1))
-        part[u, 1, :, cm] = add2(part[u, 1, :, cm], ra[u, 1]).astype(BF16)
-        send(part.at[u, :, :, cm], rb.at[u, 1], ss, rr, "head", dev1(-1))
-
-    def s_a2(u):
+
+        def total(v):
+            a = add2(part[u, :, v, c1], ra[u, 0, :, v])
+            return a + ra[u, 1, :, v].astype(F32)
+            return a + add2(ra[u, 1, :, v], ra[u, 2, :, v])
+
+        part[u, :, far_v, c1] = total(far_v).astype(BF16)
+        send(part.at[u, :, far_v, c1], rb.at[u], ss, rr, "head", dev2(2))
+        mine_sum[u] = total(own_v)
+
+    def s_fin(u):
         wait(rb.at[u], rs_r.at[1, u])
-        ss, rr = rs_s.at[2, u], rs_r.at[2, u]
-        part[u, :, :, c1] = (add2(part[u, :, :, c1], rb[u, 0]) + rb[u, 1].astype(F32)).astype(BF16)
-        send(part.at[u, 0, far_v, c1], rc.at[u, 0], ss, rr, "head", dev2(1))
-        send(part.at[u, 1, far_v, c1], rc.at[u, 1], ss, rr, "head", dev2(-1))
-
-    def s_b2(u):
-        wait(rc.at[u], rs_r.at[2, u])
-        ss, rr = rs_s.at[3, u], rs_r.at[3, u]
-        send(rc.at[u, 0], rd.at[u, 0], ss, rr, "head", dev2(1))
-        send(rc.at[u, 1], rd.at[u, 1], ss, rr, "head", dev2(-1))
-
-    def s_fin(u):
-        wait(rd.at[u], rs_r.at[3, u])
         k, p = u // 3, u % 3
         for e in range(2):
-            qkv[p, 2 * k + e] = add2(part[u, e, own_v, c1], rd[u, e]).astype(BF16)
+            qkv[p, 2 * k + e] = (mine_sum[u, e] + rb[u, e].astype(F32)).astype(BF16)
 
     def prepare():
         node_col = iota((128, 128), 0).astype(F32) + (128 * h).astype(F32)
@@ -365,11 +369,12 @@
         live = iota((256, PIECE), 1) + PIECE * c < clen[r]
         soften(r, jnp.where(live, s, NEG), kv_v[1, r, here, :])
 
-    start_att = 9 + 4 * LAG
+    start_att = 9 + (3) * LAG
     last = start_att + 8
 
     def body(it, carry):
-        for lag, stage in ((4 * LAG, s_fin), (3 * LAG, s_b2), (2 * LAG, s_a2), (LAG, s_b1)):
+        stages = ((3 * LAG, s_fin), (2 * LAG, s_sum), (LAG, s_b1))
+        for lag, stage in stages:
             @pl.when((it >= lag) & (it < UNITS + lag))
             def _(lag=lag, stage=stage):
                 stage(it - lag)
@@ -385,18 +390,14 @@
             def _():
                 x_mate()
 
-            @pl.when(it == 3)
+            @pl.when((it == 3) | (it == 6) | (it == 9))
             def _():
-                x_relay(1)
-
-            @pl.when(it == 6)
-            def _():
-                x_relay(2)
-
-            @pl.when(it == 9)
-            def _():
-                wait(xbuf.at[3, 0], x_r.at[5])
-                wait(xbuf.at[3, 1], x_r.at[6])
+                k = it // 3
+                wait(xbuf.at[k, 0], x_r.at[2 * k - 1])
+                wait(xbuf.at[k, 1], x_r.at[2 * k])
+                @pl.when(it < 9)
+                def _():
+                    x_relay(k)
 
             s_matmul(it)
 
@@ -404,18 +405,14 @@
         def _():
             prepare()
 
-        @pl.when(it == 6)
+        @pl.when(it == 8)
         def _():
             wo_c.wait()
-            ag_own(wo_v, w_s, w_r)
-
-        @pl.when(it == 11)
+            wo_own()
+
+        @pl.when(it == start_att + 4)
         def _():
-            ag_near(wo_v, w_s, w_r, HEAD // 2)
-
-        @pl.when(it == start_att + 5)
-        def _():
-            ag_far(wo_v, w_s, w_r)
+            wo_mate()
 
         @pl.when(it == start_att)
         def _():
@@ -431,25 +428,21 @@
     lax.fori_loop(0, last, body, 0)
 
     def drain_rs():
-        for i in (0, 1, 3, 4):
+        for i in range(5):
             wait(xbuf.at[0, 0], x_s.at[i])
-        wait(pack, x_s.at[2])
-        for i in (5, 6, 7, 8):
+        for i in range(5, 9):
             wait(xbuf.at[0, 0, pl.ds(0, 64)], x_s.at[i])
-        ag_drain(wo_v, w_s, HEAD // 2)
-        for i, c in ((0, tz(0, True)), (4, tz(-1, True)), (5, tz(1, True)), (6, tz(2, True))):
-            wait(wo_v.at[c], w_r.at[i])
+        wo_rest()
         for p in range(3):
             wait(wa.at[p, sent], p_s.at[p, 0])
             wait(wb.at[p, sent], p_s.at[p, 1])
 
         def drain(u, carry):
-            for k, ref in enumerate((ra, rb, rc, rd)):
+            for k, ref in enumerate((ra.at[:, 2], rb, ra.at[:, 0:2])):
                 wait(ref.at[u], rs_s.at[k, u])
             return carry
 
         lax.fori_loop(0, UNITS, drain, 0)
-
 
     k_n, v_n = in_nodes(1).astype(BF16), in_nodes(2).astype(BF16)
     outs = []
@@ -477,7 +470,6 @@
         akv_ref[1, r] = mm(pick, v_n).astype(BF16)
     for d in range(1, 8):
         wait(res.at[(t - d + 8) % 8, h], aa_r.at[d - 1])
-
 
     steps = (0, -1, 1, 2)
 
@@ -569,12 +561,11 @@
             v((3, KW, COLS - ASPLIT), BF16), v((2, 2, 2048, COLS), BF16), v((4, 2, 128, 3 * KW), BF16),
             v((128, 3 * KW), BF16),
             v((8, HEAD, COLS), BF16), v((UNITS, 2, 2, 4, 16, COLS), BF16),
-            v((UNITS, 2, 2, 16, COLS), BF16), v((UNITS, 2, 2, 2, 16, COLS), BF16),
-            v((UNITS, 2, 16, COLS), BF16), v((UNITS, 2, 16, COLS), BF16),
+            v((UNITS, 3, 2, 2, 16, COLS), BF16), v((UNITS, 2, 16, COLS), BF16), v((UNITS, 2, 16, COLS), F32),
             v((3, 8, 16, COLS), BF16), v((ROWS, ROWS), BF16), v((128, 128), BF16), v((128, 128), BF16),
             v((2, NODES, NODES), F32), v((2, 256, COLS), BF16), v((2, 256, COLS), F32),
             v((2, 256, 128), F32), v((2, 256, 128), F32), v((8, 16, COLS), BF16), v((8, 16, 16, COLS), BF16),
-            dma((8,)), dma((9,)), dma((7,)), dma((8,)), dma((7,)), dma((3, 2)), dma((3, 2)), dma((4, UNITS)), dma((4, UNITS)),
+            dma((8,)), dma((9,)), dma((7,)), dma((7,)), dma((7,)), dma((3, 2)), dma((3, 2)), dma((3, UNITS)), dma((3, UNITS)),
             dma((7,)), dma((7,)), dma((2, 2)), dma((2, 2)), dma((2, 2)), dma((2,)),
             dma((2, 4, 2)), dma((2, 4, 2)), dma((2, 4, 2)), dma((2, 4)),
         ],

time: 138 us -> 107 us (0.78)
  Pallas kernels: 134 us -> 103 us
    pallas_call x1, Pallas kernels: 134 us -> 103 us  [on_device(): pl.pallas_call(kernel, out_shape=(jax.ShapeDtypeStruct((HEAD, ROWS), BF16...]
where the time goes in v3:
time: 107 us
  Pallas kernels  103 us (96%)
  local copies, waits for them, and re-layouts  3 us (3%)
    pallas_call x1, Pallas kernels, on_device(): pl.pallas_call(kernel, out_shape=(jax.ShapeDtypeStruct((HEAD, ROWS), BF16...  103 us
    unnamed x2, local copies, waits for them, and re-layouts  3 us

profile of v3, /device:TPU:0, one launch (start us, length us, event | category | flops | bytes accessed | tf_op | source)
XLA Modules:
  0.0 107.0 jit_solution(18232306803939697344)
XLA Ops:
  0.6 103.4 %tree_verify.1 = (bf16[224,256]{1,0:T(8,128)(2,1)}, bf16[2,2,8,896]{3,2,1,0:T(8,128)(2,1)}) custom-call(bf16[256,7168]{1,0:T(8,128)(2,1)} %stream_h.1, s32[16,128]{1,0:T(8,128)} %bitcast.11, bf16[56,128]{1,0:T(8,128)(2,1)} %bitcast.10, bf16[3,448,896]{2,1,0:T(8,128)(2,1)} %bitcast.6, bf16[7168,128]{1,0:T(8,128)(2,1)} %adown_h.1, bf16[3,8,896]{2,1,0:T(8,128)(2,1)} %bitcast.9, ...), custom_call_target="tpu_custom_call" | custom-call | tf_op jit(solution)/shard_map/tree_verify/pallas_call | solution.py:550
  104.0 1.6 %copy.15 = bf16[256,224]{0,1:T(8,128)(2,1)} copy(bf16[256,224]{0,1:T(8,128)(2,1)} %bitcast.8) | data formatting | bytes 229376
  105.6 1.4 %copy.16 = bf16[2,2,8,896]{3,2,1,0:T(8,128)(2,1)} copy(bf16[2,2,8,896]{3,2,1,0:T(8,128)(2,1)} %get-tuple-element.9) | data formatting | bytes 114688

commit v4 on v3

--- a/solution.py
+++ b/solution.py
@@ -21,9 +21,11 @@
 KW = 512
 UNITS = 12
 LAG = 3
-ASPLIT = 512
+SPLITS = (512, 384, 512)
 SENT = 464
-PIECE = 512
+PIECE = 1024
+WIN = 512
+SPLIT = 384
 NEG = float("-inf")
 NT = (((1,), (1,)), ((), ()))
 
@@ -56,7 +58,7 @@
     stream_h, nodes, gain, wqkv_h, adown_h, aup, kv_h, clen, parents, accepted, wo_h,
     out_ref, akv_ref,
     stream_v, gain32, adown_v, low_acc, rstd_v, wbuf, wa, wb, kv_v, xbuf, pack, wo_v, part,
-    ra, rb, mine_sum, qkv, sort_p, node_q, node_qt, anc_v, qbd, acc_v, m_v, l_v, att, res,
+    ra, rb, mine_sum, qkv, sort_p, node_q, node_qt, anc_v, qbd, acc_v, m_v, l_v, kn_v, vn_v, att, res,
     ld, x_s, x_r, w_s, w_r, p_s, p_r, rs_s, rs_r, aa_s, aa_r, g1_s, g1_r, g2_s, g2_r, g3_s, g3_r, g4_s, g4_r,
 ):
     t = lax.axis_index("tok")
@@ -124,11 +126,18 @@
     wo_c.start()
     kv_c = pltpu.make_async_copy(kv_h, kv_v, ld.at[7])
 
+    def shares(p):
+        cut = SPLITS[p]
+        return (
+            (pl.ds(0, cut), wa.at[:, :, pl.ds(0, cut)], dev_a),
+            (pl.ds(cut, COLS - cut), wb.at[:, :, pl.ds(0, COLS - cut)], dev_b),
+        )
+
     blank = jnp.zeros((48, COLS), BF16)
     for p in range(3):
         for lo in (0, 464):
-            wa[p, lo:lo + 48, :] = blank[:, :ASPLIT]
-            wb[p, lo:lo + 48, :] = blank[:, ASPLIT:]
+            wa[p, lo:lo + 48, :] = blank[:, :512]
+            wb[p, lo:lo + 48, :] = blank[:, :512]
 
     bar = pltpu.get_barrier_semaphore()
     for d in range(1, 8):
@@ -159,10 +168,16 @@
         for p in range(3):
             wait(wa.at[p, sent], p_r.at[p, 0])
             wait(wb.at[p, sent], p_r.at[p, 1])
-            wait(wa.at[p, sent], p_s.at[p, 0])
-            wait(wb.at[p, sent], p_s.at[p, 1])
+            for i, (_, dst, _) in enumerate(shares(p)):
+                wait(dst.at[p, sent], p_s.at[p, i])
         out_ref[...] = jnp.zeros(out_ref.shape, BF16)
         akv_ref[...] = jnp.zeros(akv_ref.shape, BF16)
+
+    pl.semaphore_wait(bar, 13)
+    w_c.wait()
+    for p in range(3):
+        for i, (cols, dst, to) in enumerate(shares(p)):
+            send(wbuf.at[p, sent, cols], dst.at[p, sent], p_s.at[p, i], p_r.at[p, i], "head", to)
 
     for r in range(4):
         loads[r].wait()
@@ -177,14 +192,6 @@
         acc = lax.fori_loop(0, 7, sq, jnp.zeros((64, 128), F32))
         mean = jnp.sum(acc, axis=1, keepdims=True) * (1.0 / WIDTH)
         rstd_v[pl.ds(64 * r, 64), :] = jnp.broadcast_to(lax.rsqrt(mean + 1e-5), (64, 128))
-    pl.semaphore_wait(bar, 13)
-    w_c.wait()
-    for p in range(3):
-        src = wbuf.at[p, sent, pl.ds(0, ASPLIT)]
-        send(src, wa.at[p, sent], p_s.at[p, 0], p_r.at[p, 0], "head", dev_a)
-        src = wbuf.at[p, sent, pl.ds(ASPLIT, COLS - ASPLIT)]
-        send(src, wb.at[p, sent], p_s.at[p, 1], p_r.at[p, 1], "head", dev_b)
-
     kv_c.start()
     adown_c.wait()
     low_acc[...] = jnp.zeros((ROWS, RANK), F32)
@@ -276,10 +283,23 @@
     def s_matmul(u):
         k, p = u // 3, u % 3
         base = mm(xbuf[k, :, :, 0:KW].reshape(256, KW), wbuf[p])
-        a = base[:, :ASPLIT] + mm(xbuf[k, :, :, KW:2 * KW].reshape(256, KW), wa[p])
-        part[u, :, :, :, :, 0:ASPLIT] = a.astype(BF16).reshape(2, 2, 4, 16, ASPLIT)
-        b = base[:, ASPLIT:] + mm(xbuf[k, :, :, 2 * KW:3 * KW].reshape(256, KW), wb[p])
-        part[u, :, :, :, :, ASPLIT:COLS] = b.astype(BF16).reshape(2, 2, 4, 16, COLS - ASPLIT)
+        near_a = xbuf[k, :, :, KW:2 * KW].reshape(256, KW)
+        near_b = xbuf[k, :, :, 2 * KW:3 * KW].reshape(256, KW)
+
+        def finish(cut):
+            a = base[:, :cut] + mm(near_a, wa[p, :, 0:cut])
+            part[u, :, :, :, :, 0:cut] = a.astype(BF16).reshape(2, 2, 4, 16, cut)
+            b = base[:, cut:] + mm(near_b, wb[p, :, 0:COLS - cut])
+            part[u, :, :, :, :, cut:COLS] = b.astype(BF16).reshape(2, 2, 4, 16, COLS - cut)
+
+        @pl.when(p == 1)
+        def _():
+            finish(SPLITS[1])
+
+        @pl.when(p != 1)
+        def _():
+            finish(SPLITS[0])
+
         s_a1(u)
 
     def s_a1(u):
@@ -343,34 +363,41 @@
     def in_nodes(p):
         return mm(node_qt[...], qkv[p].reshape(128, COLS))
 
+    def heads_in(pair):
+        return (iota((NODES, WIN), 1) + SPLIT * pair) // HEAD
+
     def spread_queries():
         q = in_nodes(0)
-        head_of = iota((NODES, COLS), 1) // HEAD
-        for r in range(2):
-            qr = q[NODES * r:NODES * r + NODES]
-            for j in range(LOCAL_HEADS):
-                qbd[r, NODES * j:NODES * j + NODES, :] = jnp.where(head_of == j, qr, 0.0).astype(BF16)
+        for pair in range(2):
+            head_of = heads_in(pair)
+            for r in range(2):
+                qr = q[NODES * r:NODES * r + NODES, SPLIT * pair:SPLIT * pair + WIN]
+                for j in range(2):
+                    qbd[pair, r, NODES * j:NODES * j + NODES, :] = jnp.where(
+                        head_of == 2 * pair + j, qr, 0.0
+                    ).astype(BF16)
 
     scale = HEAD ** -0.5
 
-    def soften(r, s, values):
-        m_old = m_v[r]
+    def soften(pair, r, s, values):
+        m_old = m_v[pair, r]
         m_new = jnp.maximum(m_old, jnp.broadcast_to(jnp.max(s, axis=1, keepdims=True), m_old.shape))
         shrink = jnp.exp(m_old - m_new)
         e = jnp.exp(s - m_new[:, 0:1])
-        m_v[r] = m_new
-        l_v[r] = l_v[r] * shrink + jnp.broadcast_to(jnp.sum(e, axis=1, keepdims=True), m_old.shape)
-        acc_v[r] = acc_v[r] * shrink[:, 0:1] + mm(e.astype(BF16), values)
-
-    def cache_piece(i):
-        r, c = i // 4, i % 4
+        m_v[pair, r] = m_new
+        l_v[pair, r] = l_v[pair, r] * shrink + jnp.broadcast_to(jnp.sum(e, axis=1, keepdims=True), m_old.shape)
+        acc_v[pair, r] = acc_v[pair, r] * shrink[:, 0:1] + mm(e.astype(BF16), values)
+
+    def cache_piece(pair, i):
+        r, c = i // 2, i % 2
         here = pl.ds(pl.multiple_of(PIECE * c, PIECE), PIECE)
-        s = lax.dot_general(qbd[r], kv_v[0, r, here, :], NT, preferred_element_type=F32) * scale
-        live = iota((256, PIECE), 1) + PIECE * c < clen[r]
-        soften(r, jnp.where(live, s, NEG), kv_v[1, r, here, :])
+        cols = pl.ds(SPLIT * pair, WIN)
+        s = lax.dot_general(qbd[pair, r], kv_v[0, r, here, cols], NT, preferred_element_type=F32) * scale
+        live = iota((128, PIECE), 1) + PIECE * c < clen[r]
+        soften(pair, r, jnp.where(live, s, NEG), kv_v[1, r, here, cols])
 
     start_att = 9 + (3) * LAG
-    last = start_att + 8
+    last = start_att + 4
 
     def body(it, carry):
         stages = ((3 * LAG, s_fin), (2 * LAG, s_sum), (LAG, s_b1))
@@ -381,10 +408,11 @@
 
         @pl.when(it < UNITS)
         def _():
-            @pl.when(it < 3)
-            def _():
-                wait(wa.at[it, sent], p_r.at[it, 0])
-                wait(wb.at[it, sent], p_r.at[it, 1])
+            for p in range(3):
+                @pl.when(it == p)
+                def _(p=p):
+                    for i, (_, dst, _) in enumerate(shares(p)):
+                        wait(dst.at[p, sent], p_r.at[p, i])
 
             @pl.when(it == 0)
             def _():
@@ -410,7 +438,7 @@
             wo_c.wait()
             wo_own()
 
-        @pl.when(it == start_att + 4)
+        @pl.when(it == start_att + 3)
         def _():
             wo_mate()
 
@@ -419,9 +447,9 @@
             kv_c.wait()
             spread_queries()
 
-        @pl.when((it >= start_att) & (it < start_att + 8))
-        def _():
-            cache_piece(it - start_att)
+        @pl.when(it >= start_att)
+        def _():
+            cache_piece(0, it - start_att)
 
         return carry
 
@@ -434,8 +462,8 @@
             wait(xbuf.at[0, 0, pl.ds(0, 64)], x_s.at[i])
         wo_rest()
         for p in range(3):
-            wait(wa.at[p, sent], p_s.at[p, 0])
-            wait(wb.at[p, sent], p_s.at[p, 1])
+            for i, (_, dst, _) in enumerate(shares(p)):
+                wait(dst.at[p, sent], p_s.at[p, i])
 
         def drain(u, carry):
             for k, ref in enumerate((ra.at[:, 2], rb, ra.at[:, 0:2])):
@@ -444,32 +472,36 @@
 
         lax.fori_loop(0, UNITS, drain, 0)
 
-    k_n, v_n = in_nodes(1).astype(BF16), in_nodes(2).astype(BF16)
-    outs = []
-    for r in range(2):
-        rows = slice(NODES * r, NODES * r + NODES)
-        s = lax.dot_general(qbd[r], k_n[rows], NT, preferred_element_type=F32) * scale
-        keep = jnp.concatenate([anc_v[r]] * LOCAL_HEADS, axis=0) > 0.5
-        soften(r, jnp.where(keep, s, NEG), v_n[rows])
-        norm = acc_v[r] / l_v[r][:, 0:1]
-        head_of = iota((NODES, COLS), 1) // HEAD
-        o = jnp.zeros((NODES, COLS), F32)
-        for j in range(LOCAL_HEADS):
-            o = jnp.where(head_of == j, norm[NODES * j:NODES * j + NODES], o)
-        outs.append(o.astype(BF16))
-    att[...] = mm(node_q[...], jnp.concatenate(outs, axis=0)).astype(BF16).reshape(8, 16, COLS)
-
-    for d in range(1, 8):
-        to = (t + d) % 8
-        send(att.at[slot_of(to)], res.at[t, h], aa_s.at[d - 1], aa_r.at[d - 1], "tok", to)
-    res[t, h] = att[core]
-    for r in range(2):
-        col = column_of(accepted[r:r + 1, :].astype(F32)) + float(NODES * r)
-        pick = one(iota((8, 128), 1).astype(F32) == jnp.broadcast_to(col, (8, 128)))
-        akv_ref[0, r] = mm(pick, k_n).astype(BF16)
-        akv_ref[1, r] = mm(pick, v_n).astype(BF16)
-    for d in range(1, 8):
-        wait(res.at[(t - d + 8) % 8, h], aa_r.at[d - 1])
+    kn_v[...] = in_nodes(1).astype(BF16)
+    vn_v[...] = in_nodes(2).astype(BF16)
+
+    def tree(pair):
+        outs = []
+        head_of = heads_in(pair)
+        for r in range(2):
+            rows = pl.ds(NODES * r, NODES)
+            cols = pl.ds(SPLIT * pair, WIN)
+            s = lax.dot_general(qbd[pair, r], kn_v[rows, cols], NT, preferred_element_type=F32) * scale
+            keep = jnp.concatenate([anc_v[r]] * 2, axis=0) > 0.5
+            soften(pair, r, jnp.where(keep, s, NEG), vn_v[rows, cols])
+            norm = acc_v[pair, r] / l_v[pair, r][:, 0:1]
+            outs.append(jnp.where(head_of == 2 * pair, norm[0:NODES], norm[NODES:2 * NODES]))
+        return jnp.concatenate(outs, axis=0).astype(BF16)
+
+    lanes = (pl.ds(0, SPLIT), pl.ds(SPLIT, WIN))
+
+    def home_sends(c):
+        for d in range(1, 8):
+            to = (t + d) % 8
+            send(
+                att.at[slot_of(to), :, lanes[c]], res.at[t, h, :, lanes[c]],
+                aa_s.at[c, d - 1], aa_r.at[c, d - 1], "tok", to,
+            )
+        res[t, h, :, lanes[c]] = att[core, :, lanes[c]]
+
+    def home_waits(c):
+        for d in range(1, 8):
+            wait(res.at[(t - d + 8) % 8, h, :, lanes[c]], aa_r.at[c, d - 1])
 
     steps = (0, -1, 1, 2)
 
@@ -478,67 +510,120 @@
             return ((y + j + 4) % 4) * 4 + (x + i + 4) % 4
         return ((y + i + 4) % 4) * 4 + (x + j + 4) % 4
 
-    def blk(hf, i, j, part_of=None):
+    def blk(c, hf, i, j, part_of=None):
         lo, n = (4 * hf, 4) if part_of is None else (4 * hf + 2 * part_of, 2)
-        return res.at[pl.ds(lo, n), slot(hf, i, j)]
+        return res.at[pl.ds(lo, n), slot(hf, i, j), :, lanes[c]]
 
     def dev(hf, axis, d):
         return slot(hf, d, 0) if axis == 0 else slot(hf, 0, d)
 
-    def first_sends(hf):
+    def cross_sends(c, hf, n_i):
+        b = blk(c, hf, steps[n_i], 0)
         for n, d in enumerate((1, -1)):
-            send(blk(hf, 0, 0), blk(hf, 0, 0), g1_s.at[hf, n], g1_r.at[hf, n], "head", dev(hf, 0, d))
-
-    def cross_sends(hf, n_i):
+            send(b, b, g3_s.at[c, hf, n_i, n], g3_r.at[c, hf, n_i, n], "head", dev(hf, 1, d))
+
+    def cross_forward(c, n_i):
         i = steps[n_i]
-        for n, d in enumerate((1, -1)):
-            send(blk(hf, i, 0), blk(hf, i, 0), g3_s.at[hf, n_i, n], g3_r.at[hf, n_i, n], "head", dev(hf, 1, d))
-
-    def cross_forward(hf, n_i):
-        i = steps[n_i]
-        for n, d in enumerate((1, -1)):
-            wait(blk(hf, i, -d), g3_r.at[hf, n_i, n])
-            send(blk(hf, i, -d, n), blk(hf, i, -d, n), g4_s.at[hf, n_i, n], g4_r.at[hf, n_i], "head", dev(hf, 1, d))
-
-    for hf in range(2):
-        first_sends(hf)
-    for hf in range(2):
-        cross_sends(hf, 0)
-    for hf in range(2):
-        for n, d in enumerate((1, -1)):
-            wait(blk(hf, -d, 0), g1_r.at[hf, n])
-            send(blk(hf, -d, 0, n), blk(hf, -d, 0, n), g2_s.at[hf, n], g2_r.at[hf], "head", dev(hf, 0, d))
-            cross_sends(hf, 1 + n)
-    for hf in range(2):
-        cross_forward(hf, 0)
-    for hf in range(2):
-        wait(blk(hf, 2, 0), g2_r.at[hf])
-        cross_sends(hf, 3)
-    for n_i in (1, 2, 3):
         for hf in range(2):
-            cross_forward(hf, n_i)
-
+            for n, d in enumerate((1, -1)):
+                wait(blk(c, hf, i, -d), g3_r.at[c, hf, n_i, n])
+                b = blk(c, hf, i, -d, n)
+                send(b, b, g4_s.at[c, hf, n_i, n], g4_r.at[c, hf, n_i], "head", dev(hf, 1, d))
+
+    def gather_first(c):
+        for hf in range(2):
+            b = blk(c, hf, 0, 0)
+            for n, d in enumerate((1, -1)):
+                send(b, b, g1_s.at[c, hf, n], g1_r.at[c, hf, n], "head", dev(hf, 0, d))
+        for hf in range(2):
+            cross_sends(c, hf, 0)
+
+    def gather_second(c):
+        for hf in range(2):
+            for n, d in enumerate((1, -1)):
+                wait(blk(c, hf, -d, 0), g1_r.at[c, hf, n])
+                b = blk(c, hf, -d, 0, n)
+                send(b, b, g2_s.at[c, hf, n], g2_r.at[c, hf], "head", dev(hf, 0, d))
+                cross_sends(c, hf, 1 + n)
+
+    def gather_third(c):
+        for hf in range(2):
+            wait(blk(c, hf, 2, 0), g2_r.at[c, hf])
+            cross_sends(c, hf, 3)
+
+    def gather_end(c):
+        for hf in range(2):
+            for n_i in range(4):
+                wait(blk(c, hf, steps[n_i], 2), g4_r.at[c, hf, n_i])
+
+    def project(c):
+        total = jnp.zeros((HEAD, ROWS), F32)
+        width = (SPLIT, WIN)[c]
+        for s in range(8):
+            total = total + lax.dot_general(
+                wo_v[s, :, lanes[c]], res[s, :, :, lanes[c]].reshape(ROWS, width), NT, preferred_element_type=F32
+            )
+        return total
+
+    o0 = tree(0)
+    att[:, :, 0:SPLIT] = mm(node_q[...], o0[:, 0:SPLIT]).astype(BF16).reshape(8, 16, SPLIT)
+    home_sends(0)
+
+    def second(i, carry):
+        cache_piece(1, i)
+        return carry
+
+    lax.fori_loop(0, 4, second, 0)
+    home_waits(0)
+    gather_first(0)
+    o1 = tree(1)
+    first_lanes = jnp.where(
+        iota((128, 128), 1) < 2 * HEAD - SPLIT, o0[:, SPLIT:WIN].astype(F32), o1[:, 0:128].astype(F32)
+    ).astype(BF16)
+    o1 = jnp.concatenate([first_lanes, o1[:, 128:WIN]], axis=1)
+    att[:, :, SPLIT:COLS] = mm(node_q[...], o1).astype(BF16).reshape(8, 16, WIN)
+    home_sends(1)
+    gather_second(0)
+    for r in range(2):
+        col = column_of(accepted[r:r + 1, :].astype(F32)) + float(NODES * r)
+        pick = one(iota((8, 128), 1).astype(F32) == jnp.broadcast_to(col, (8, 128)))
+        akv_ref[0, r] = mm(pick, kn_v[...]).astype(BF16)
+        akv_ref[1, r] = mm(pick, vn_v[...]).astype(BF16)
+    home_waits(1)
+    gather_first(1)
+    cross_forward(0, 0)
+    gather_third(0)
+    cross_forward(0, 1)
+    cross_forward(0, 2)
+    gather_second(1)
+    cross_forward(0, 3)
+    cross_forward(1, 0)
+    gather_third(1)
     drain_rs()
-    for hf in range(2):
-        for n_i in range(4):
-            wait(blk(hf, steps[n_i], 2), g4_r.at[hf, n_i])
-
-    total = jnp.zeros((HEAD, ROWS), F32)
-    for s in range(8):
-        total = total + lax.dot_general(
-            wo_v[s], res[s].reshape(ROWS, COLS), NT, preferred_element_type=F32
-        )
+    gather_end(0)
+    cross_forward(1, 1)
+    cross_forward(1, 2)
+    half = project(0)
+    cross_forward(1, 3)
+    gather_end(1)
+    total = half + project(1)
     out_ref[...] = mm(total.astype(BF16), sort_p[...]).astype(BF16)
 
-    for d in range(1, 8):
-        wait(att.at[0], aa_s.at[d - 1])
-    for hf in range(2):
-        for n in range(2):
-            wait(blk(hf, 0, 0), g1_s.at[hf, n])
-            wait(blk(hf, 0, 0, 0), g2_s.at[hf, n])
-            for n_i in range(4):
-                wait(blk(hf, 0, 0), g3_s.at[hf, n_i, n])
-                wait(blk(hf, 0, 0, 0), g4_s.at[hf, n_i, n])
+    for c in range(2):
+        for d in range(1, 8):
+            wait(att.at[0, :, lanes[c]], aa_s.at[c, d - 1])
+        for hf in range(2):
+            for n in range(2):
+                wait(blk(c, hf, 0, 0), g1_s.at[c, hf, n])
+                wait(blk(c, hf, 0, 0, 0), g2_s.at[c, hf, n])
+                for n_i in range(4):
+                    wait(blk(c, hf, 0, 0), g3_s.at[c, hf, n_i, n])
+                    wait(blk(c, hf, 0, 0, 0), g4_s.at[c, hf, n_i, n])
+
+
+def hand_out(a_ref, b_ref, a_out, b_out):
+    a_out[...] = a_ref[...]
+    b_out[...] = b_ref[...]
 
 
 def on_device(stream, row_tree_nodes, gain, wqkv, adown, aup, kv, clen, parents, accepted, wo):
@@ -557,17 +642,17 @@
         out_specs=(vm, vm),
         scratch_shapes=[
             v((ROWS, WIDTH), BF16), v((56, 128), F32), v((WIDTH, RANK), BF16), v((ROWS, RANK), F32),
-            v((ROWS, 128), F32), v((3, KW, COLS), BF16), v((3, KW, ASPLIT), BF16),
-            v((3, KW, COLS - ASPLIT), BF16), v((2, 2, 2048, COLS), BF16), v((4, 2, 128, 3 * KW), BF16),
+            v((ROWS, 128), F32), v((3, KW, COLS), BF16), v((3, KW, 512), BF16),
+            v((3, KW, 512), BF16), v((2, 2, 2048, COLS), BF16), v((4, 2, 128, 3 * KW), BF16),
             v((128, 3 * KW), BF16),
             v((8, HEAD, COLS), BF16), v((UNITS, 2, 2, 4, 16, COLS), BF16),
             v((UNITS, 3, 2, 2, 16, COLS), BF16), v((UNITS, 2, 16, COLS), BF16), v((UNITS, 2, 16, COLS), F32),
             v((3, 8, 16, COLS), BF16), v((ROWS, ROWS), BF16), v((128, 128), BF16), v((128, 128), BF16),
-            v((2, NODES, NODES), F32), v((2, 256, COLS), BF16), v((2, 256, COLS), F32),
-            v((2, 256, 128), F32), v((2, 256, 128), F32), v((8, 16, COLS), BF16), v((8, 16, 16, COLS), BF16),
+            v((2, NODES, NODES), F32), v((2, 2, 128, WIN), BF16), v((2, 2, 128, WIN), F32),
+            v((2, 2, 128, 128), F32), v((2, 2, 128, 128), F32), v((128, COLS), BF16), v((128, COLS), BF16), v((8, 16, COLS), BF16), v((8, 16, 16, COLS), BF16),
             dma((8,)), dma((9,)), dma((7,)), dma((7,)), dma((7,)), dma((3, 2)), dma((3, 2)), dma((3, UNITS)), dma((3, UNITS)),
-            dma((7,)), dma((7,)), dma((2, 2)), dma((2, 2)), dma((2, 2)), dma((2,)),
-            dma((2, 4, 2)), dma((2, 4, 2)), dma((2, 4, 2)), dma((2, 4)),
+            dma((2, 7)), dma((2, 7)), dma((2, 2, 2)), dma((2, 2, 2)), dma((2, 2, 2)), dma((2, 2)),
+            dma((2, 2, 4, 2)), dma((2, 2, 4, 2)), dma((2, 2, 4, 2)), dma((2, 2, 4)),
         ],
         compiler_params=pltpu.CompilerParams(
             collective_id=0, has_side_effects=True, vmem_limit_bytes=67043328
@@ -577,6 +662,13 @@
         stream, row_tree_nodes.reshape(16, 128), gain.reshape(56, 128), jnp.transpose(wqkv, (1, 0, 2)),
         adown, jnp.transpose(aup, (1, 0, 2)), kv, clen, parents, accepted, jnp.transpose(wo),
     )
+    out_t, akv = pl.pallas_call(
+        hand_out,
+        out_shape=(jax.ShapeDtypeStruct(out_t.shape, BF16), jax.ShapeDtypeStruct(akv.shape, BF16)),
+        in_specs=[vm, vm],
+        out_specs=(vm, vm),
+        name="hand_out",
+    )(out_t, akv)
     return jnp.transpose(out_t), akv
 
 

time: 107 us -> 100 us (0.935)
  Pallas kernels: 103 us -> 98.8 us
  local copies, waits for them, and re-layouts: 3 us -> 0 us
    pallas_call x1, Pallas kernels: 103 us -> 97.2 us  [on_device(): pl.pallas_call(kernel, out_shape=(jax.ShapeDtypeStruct((HEAD, ROWS), BF16...]
    unnamed x2 -> x0, local copies, waits for them, and re-layouts: 3 us -> none
    pallas_call x0 -> x1, Pallas kernels: none -> 1.57 us  [on_device(): pl.pallas_call(hand_out, out_shape=(jax.ShapeDtypeStruct(out_t.shape, BF1...]
where the time goes in v4:
time: 100 us; the launch traced here: 99.4 us
  Pallas kernels  98.8 us (99%)
    pallas_call x1, Pallas kernels, on_device(): pl.pallas_call(kernel, out_shape=(jax.ShapeDtypeStruct((HEAD, ROWS), BF16...  97.2 us

profile of v4, /device:TPU:0, one launch (start us, length us, event | category | flops | bytes accessed | tf_op | source)
XLA Modules:
  0.0 99.4 jit_solution(899052049151379056)
XLA Ops:
  0.6 97.2 %tree_verify.1 = (bf16[224,256]{1,0:T(8,128)(2,1)}, bf16[2,2,8,896]{3,2,1,0:T(8,128)(2,1)}) custom-call(bf16[256,7168]{1,0:T(8,128)(2,1)} %stream_h.1, s32[16,128]{1,0:T(8,128)} %bitcast.10, bf16[56,128]{1,0:T(8,128)(2,1)} %bitcast.9, bf16[3,448,896]{2,1,0:T(8,128)(2,1)} %bitcast.6, bf16[7168,128]{1,0:T(8,128)(2,1)} %adown_h.1, bf16[3,8,896]{2,1,0:T(8,128)(2,1)} %bitcast.8, ...), custom_call_target="tpu_custom_call" | custom-call | tf_op jit(solution)/shard_map/tree_verify/pallas_call | solution.py:635
  97.8 1.6 %hand_out.1 = (bf16[224,256]{1,0:T(8,128)(2,1)}, bf16[2,2,8,896]{3,2,1,0:T(8,128)(2,1)}) custom-call(bf16[224,256]{1,0:T(8,128)(2,1)} %get-tuple-element.6.a_ref, bf16[2,2,8,896]{3,2,1,0:T(8,128)(2,1)} %get-tuple-element.7.b_ref), custom_call_target="tpu_custom_call" | custom-call | tf_op jit(solution)/shard_map/hand_out/pallas_call | solution.py:665
